TPU v7x, 256 devices: a whole 4x4x8 slice. The times are simulated.
256 devices in a mesh: gx: 64 (over y_hi, z, x), gy: 4 (over y_lo, core).
Axes of the slice: x: 4, y: 4 (y_hi: 2, y_lo: 2; y = y_hi * 2 + y_lo), z: 8, core: 2. Of those that a mesh axis runs over, the one named last changes fastest.
Arguments:
- features: bfloat16 [2048, 512, 128], P(('gx', 'gy')), may hold values from -6 to 6
- weights: bfloat16 [27, 128, 128], replicated, may hold values from -0.109375 to 0.109375
- cotangent: bfloat16 [2048, 512, 128], P(('gx', 'gy')), may hold values from -6 to 6
- occupancy: int32 [2048, 512], P(('gx', 'gy')), may hold values 0 or 1
- slot_pos: int32 [2048], P(('gx', 'gy')), may hold values from -1 to 15, as said below
Outputs:
- outputs: bfloat16 [2048, 512, 128], P(('gx', 'gy'))
- grad_input: bfloat16 [2048, 512, 128], P(('gx', 'gy'))
- grad_weight: float32 [27, 128, 128], replicated
Inputs may be any that keep to these rules, and one draw needn't show every extreme that they name: `slot_pos`: on each device the 8 slots name distinct positions of its region; live slots come first and the rest hold -1; each device has at least 4 live slots, and some device has all 8 live.
All inputs are finite; a program needn't handle non-finite values. No bound on the sum of `occupancy` on one device may be relied on, other than what follows from the above.
Results may differ from a plain program's by a relative error of at most 0.001.
Values may be sent and summed in bfloat16 or wider, within the bound.
No kernel may reach another device: no remote copies, remote signals or barrier semaphores. Data moves between devices by JAX's collectives and lax.ppermute only.
A program may use at most 64 MiB of HBM per device.

v0:
```python
import itertools
import math

import jax
import jax.numpy as jnp
from jax import lax
from jax.experimental import pallas as pl
from jax.experimental.pallas import tpu as pltpu
from jax.sharding import Mesh, PartitionSpec as P

AXES = ("y_hi", "z", "x", "y_lo", "core")
SLOTS = 8
VOX = 512
CH = 128
NX, NY, NZ = 32, 16, 16
OFFSETS = 27
KROW = 9 * CH
BLOCKS = 16
BROWS = 112
PROWS = 80
F32 = jnp.float32
BF16 = jnp.bfloat16
VMEM = pl.BlockSpec(memory_space=pltpu.VMEM)
SMEM = pl.BlockSpec(memory_space=pltpu.SMEM)
HBM = pl.BlockSpec(memory_space=pltpu.HBM)


def pin(value, space):
    return pltpu.with_memory_space_constraint(value, space)


def brick_of(pos):
    return pos >> 2, (pos >> 1) & 1, pos & 1


def mask_columns(occ_ref):
    return jnp.where(occ_ref[...] == 1, 1.0, 0.0).astype(F32).T


def start_loads(occ_hbm, slots_hbm, occ, slots, sems):
    loads = [pltpu.make_async_copy(slots_hbm.at[s], slots.at[s], sems.at[s]) for s in range(SLOTS)]
    loads.append(pltpu.make_async_copy(occ_hbm, occ, sems.at[SLOTS]))
    for load in reversed(loads):
        load.start()
    return loads


def masked_bricks(pos_ref, loads, occ, slots, put):
    loads[SLOTS].wait()
    columns = mask_columns(occ)
    for s in range(SLOTS):
        loads[s].wait()
        pos = pos_ref[s]

        @pl.when(pos >= 0)
        def _():
            keep = jnp.broadcast_to(columns[:, s : s + 1], (VOX, CH))
            put(s, brick_of(pos), jnp.where(keep > 0.5, slots[s].astype(F32), 0.0))


def fill(pos_ref, occ_hbm, slots_hbm, cells, occ, slots, sems):
    loads = start_loads(occ_hbm, slots_hbm, occ, slots, sems)

    def clear(x, carry):
        cells[x] = jnp.zeros((NY, 2, 8, CH), F32)
        return carry

    lax.fori_loop(0, NX, clear, 0)

    def put(s, at, value):
        bx, by, bz = at
        cells[pl.ds(bx * 8, 8), pl.ds(by * 8, 8), bz] = value.reshape(8, 8, 8, CH)

    masked_bricks(pos_ref, loads, occ, slots, put)


def place_kernel(pos_ref, meta_ref, occ_hbm, feat_hbm, cot_hbm, xt, even_ref, odd_ref, side_even_ref, side_odd_ref, planes, sides, occ, slots, sems):
    core, odd_x = meta_ref[0], meta_ref[3]
    sources = (cot_hbm, feat_hbm)
    loads = [start_loads(occ_hbm, sources[t], occ.at[t], slots.at[t], sems.at[t]) for t in range(2)]
    planes[...] = jnp.zeros(planes.shape, F32)
    sides[...] = jnp.zeros(sides.shape, F32)
    for t in range(2):

        def put(s, at, value):
            bx, by, bz = at
            v = value.reshape(8, 8, 8, CH)
            sides[t, by, pl.ds(bx * 8, 8), bz] = jnp.where(by == 0, v[:, 0], v[:, 7])
            for end, edge in ((0, 0), (1, 3)):

                @pl.when(bx == edge)
                def _():
                    planes[t, end, pl.ds(by * 8, 8), bz] = v[7 * end]

            if t == 1:
                xt[s] = value.T.astype(BF16)

        masked_bricks(pos_ref, loads[t], occ.at[t], slots.at[t], put)
        even_ref[t] = planes[t, 1 - odd_x].reshape(NY, NZ, CH).astype(BF16)
        odd_ref[t] = planes[t, odd_x].reshape(NY, NZ, CH).astype(BF16)
        side_even_ref[t] = sides[t, 1 - core].reshape(NX, NZ, CH).astype(BF16)
        side_odd_ref[t] = sides[t, core].reshape(NX, NZ, CH).astype(BF16)


FILL = [
    pltpu.VMEM((NX, NY, 2, 8, CH), F32),
    pltpu.VMEM((SLOTS, VOX), jnp.int32),
    pltpu.VMEM((SLOTS, VOX, CH), BF16),
    pltpu.SemaphoreType.DMA((SLOTS + 1,)),
]


def place(slot_pos, meta, occupancy, features, cotangent):
    plane = jax.ShapeDtypeStruct((2, NY, NZ, CH), BF16)
    side = jax.ShapeDtypeStruct((2, NX, NZ, CH), BF16)
    return pl.pallas_call(
        place_kernel,
        out_shape=(pltpu.VMEM((SLOTS, CH, VOX), BF16), plane, plane, side, side),
        in_specs=[SMEM, SMEM, HBM, HBM, HBM],
        out_specs=(VMEM,) * 5,
        scratch_shapes=[
            pltpu.VMEM((2, 2, NY, 2, 8, CH), F32),
            pltpu.VMEM((2, 2, NX, 2, 8, CH), F32),
            pltpu.VMEM((2, SLOTS, VOX), jnp.int32),
            pltpu.VMEM((2, SLOTS, VOX, CH), BF16),
            pltpu.SemaphoreType.DMA((2, SLOTS + 1)),
        ],
        compiler_params=pltpu.CompilerParams(vmem_limit_bytes=20 << 20),
        name="place",
    )(slot_pos, meta, *[pin(a, pltpu.HBM) for a in (occupancy, features, cotangent)])


def shifted(v):
    n = v.shape[0]
    flat = v.astype(F32).reshape(n * NZ, CH)
    z = lax.broadcasted_iota(jnp.int32, flat.shape, 0) & (NZ - 1)
    back = jnp.where(z == 0, 0.0, pltpu.roll(flat, 1, axis=0))
    ahead = jnp.where(z == NZ - 1, 0.0, pltpu.roll(flat, n * NZ - 1, axis=0))
    return [a.reshape(n, 2, 8, CH) for a in (back, flat, ahead)]


def assemble(meta_ref, t, cells_ref, side_even_ref, side_odd_ref, halo, planes=None):
    core, odd_x = meta_ref[0], meta_ref[3]

    def body(x, carry):
        for r, a in enumerate(shifted(cells_ref[x].reshape(NY, NZ, CH))):
            for bz in range(2):
                halo[r, bz, x + 1, pl.ds(1, NY)] = a[:, bz]
        return carry

    for y, ref in (((NY + 1) * (1 - core), side_even_ref), ((NY + 1) * core, side_odd_ref)):
        for r, a in enumerate(shifted(ref[t])):
            for bz in range(2):
                halo[r, bz, pl.ds(1, NX), y] = a[:, bz]
    for i, x in enumerate(((NX + 1) * (1 - odd_x), (NX + 1) * odd_x)):
        if planes is None:
            halo[:, :, x] = jnp.zeros((3, 2, NY + 2, 8, CH), F32)
        else:
            for r, a in enumerate(shifted(planes[i][t])):
                for bz in range(2):
                    halo[r, bz, x] = a[:, bz]
    lax.fori_loop(0, NX, body, 0)


def build_patches(s, pos, halo, patch_ref):
    bx, by, bz = brick_of(pos)
    for x in range(10):
        for r in range(3):
            rows = halo[r, bz, bx * 8 + x, pl.ds(by * 8, 10)]
            patch_ref[s, x, :, r * CH : (r + 1) * CH] = rows.reshape(PROWS, CH).astype(BF16)


def patch_rows(patch_ref, s, p):
    parts = [patch_ref[s, pl.ds(p, 8), pl.ds(q * 8, 64)].reshape(VOX, 3 * CH) for q in range(3)]
    return jnp.concatenate(parts, axis=1)


def patches_kernel(pos_ref, meta_ref, occ_hbm, slots_hbm, side_even_ref, side_odd_ref, even_ref, odd_ref, patch_ref, halo, cells, occ, slots, sems):
    s = pl.program_id(0)

    @pl.when(s == 0)
    def _():
        fill(pos_ref, occ_hbm, slots_hbm, cells, occ, slots, sems)
        assemble(meta_ref, 1, cells, side_even_ref, side_odd_ref, halo, (even_ref, odd_ref))

    pos = pos_ref[s]

    @pl.when(pos >= 0)
    def _():
        build_patches(s, pos, halo, patch_ref)


def weight_kernel(pos_ref, meta_ref, occ_hbm, slots_hbm, side_even_ref, side_odd_ref, xt_ref, patch_ref, total, halo, cells, occ, slots, sems):
    s = pl.program_id(0)

    @pl.when(s == 0)
    def _():
        fill(pos_ref, occ_hbm, slots_hbm, cells, occ, slots, sems)
        assemble(meta_ref, 0, cells, side_even_ref, side_odd_ref, halo)

        def clear(o, carry):
            total[pl.ds(pl.multiple_of(o * CH, CH), CH)] = jnp.zeros((CH, CH), F32)
            return carry

        lax.fori_loop(0, OFFSETS + 1, clear, 0)

    pos = pos_ref[s]

    @pl.when(pos >= 0)
    def _():
        build_patches(s, pos, halo, patch_ref)
        for p in range(3):
            terms = jnp.dot(xt_ref[0], patch_rows(patch_ref, s, p), preferred_element_type=F32)
            for k in range(9):
                row = (OFFSETS - 1 - (p * 9 + k)) * CH
                total[row : row + CH] += terms[:, k * CH : (k + 1) * CH]


def rim_kernel(pos_ref, meta_ref, even_ref, odd_ref, xt_ref, total_ref, rows, keep_ref, send_ref, rims, total):
    core, own, other, odd_x = meta_ref[0], meta_ref[1], meta_ref[2], meta_ref[3]
    for i, ref in enumerate((even_ref, odd_ref)):
        at = 1 - odd_x if i == 0 else odd_x
        for r, a in enumerate(shifted(ref[0])):
            for bz in range(2):
                rims[at, r, bz] = a[:, bz]

    def clear(o, carry):
        at = pl.ds(pl.multiple_of(o * CH, CH), CH)
        total[at] = total_ref[at]
        return carry

    lax.fori_loop(0, OFFSETS + 1, clear, 0)

    for s in range(SLOTS):
        pos = pos_ref[s]
        for end, edge in ((0, 0), (1, 3)):

            @pl.when((pos >= 0) & ((pos >> 2) == edge))
            def _():
                _, by, bz = brick_of(pos)
                for r in range(3):
                    part = rims[end, r, bz, pl.ds(by * 8, 10)]
                    rows[s, :, r * CH : (r + 1) * CH] = part.reshape(PROWS, CH).astype(BF16)
                patch = jnp.concatenate([rows[s, pl.ds(q * 8, 64)] for q in range(3)], axis=1)
                blank = jnp.zeros_like(patch)
                if end == 0:
                    left, right = xt_ref[s, :, :CH], jnp.concatenate([patch, blank], axis=0)
                else:
                    left, right = xt_ref[s, :, VOX - CH :], jnp.concatenate([blank, patch], axis=0)
                terms = jnp.dot(left, right, preferred_element_type=F32)
                for k in range(9):
                    row = (OFFSETS - 1 - (18 * end + k)) * CH
                    total[row : row + CH] += terms[:, k * CH : (k + 1) * CH]

    def emit(j, carry):
        at = pl.multiple_of((core * BLOCKS + (j ^ own)) * BROWS, 8)
        keep_ref[j] = total[pl.ds(at, BROWS)]
        at = pl.multiple_of(((1 - core) * BLOCKS + (j ^ other)) * BROWS, 8)
        send_ref[j] = total[pl.ds(at, BROWS)]
        return carry

    lax.fori_loop(0, BLOCKS, emit, 0)

PATCH_SHAPE = pltpu.VMEM((SLOTS, 10, PROWS, 3 * CH), BF16)
RIM_SHAPE = pltpu.VMEM((SLOTS, PROWS, 3 * CH), BF16)
HALO = pltpu.VMEM((3, 2, NX + 2, NY + 2, 8, CH), F32)
TOTAL = pltpu.VMEM(((OFFSETS + 1) * CH, CH), F32)


def patches(slot_pos, meta, occupancy, slots, sides, planes):
    return pl.pallas_call(
        patches_kernel,
        out_shape=PATCH_SHAPE,
        grid=(SLOTS,),
        in_specs=[SMEM, SMEM, HBM, HBM] + [VMEM] * 4,
        out_specs=VMEM,
        scratch_shapes=[HALO] + FILL,
        compiler_params=pltpu.CompilerParams(vmem_limit_bytes=28 << 20),
        cost_estimate=pl.CostEstimate(flops=0, bytes_accessed=20 << 20, transcendentals=0),
        name="patches",
    )(slot_pos, meta, pin(occupancy, pltpu.HBM), pin(slots, pltpu.HBM), *sides, *planes)


def weight_gradient(slot_pos, meta, occupancy, slots, sides, xt):
    return pl.pallas_call(
        weight_kernel,
        out_shape=(PATCH_SHAPE, TOTAL),
        grid=(SLOTS,),
        in_specs=[SMEM, SMEM, HBM, HBM] + [VMEM] * 2 + [pl.BlockSpec((1, CH, VOX), lambda s: (s, 0, 0))],
        out_specs=(VMEM, VMEM),
        scratch_shapes=[HALO] + FILL,
        compiler_params=pltpu.CompilerParams(vmem_limit_bytes=30 << 20),
        cost_estimate=pl.CostEstimate(flops=2 * 4096 * OFFSETS * CH * CH, bytes_accessed=20 << 20, transcendentals=0),
        name="weight_gradient",
    )(slot_pos, meta, pin(occupancy, pltpu.HBM), pin(slots, pltpu.HBM), *sides, xt)


def rim_terms(slot_pos, meta, planes, xt, total):
    half = pltpu.VMEM((BLOCKS, BROWS, CH), F32)
    return pl.pallas_call(
        rim_kernel,
        out_shape=(RIM_SHAPE, half, half),
        in_specs=[SMEM, SMEM] + [VMEM] * 4,
        out_specs=(VMEM, VMEM, VMEM),
        scratch_shapes=[pltpu.VMEM((2, 3, 2, NY + 2, 8, CH), F32), TOTAL],
        compiler_params=pltpu.CompilerParams(vmem_limit_bytes=20 << 20),
        name="rim_terms",
    )(slot_pos, meta, *planes, xt, total)


def flip_kernel(w_ref, out_ref):
    for o in range(OFFSETS):
        out_ref[o * CH : (o + 1) * CH] = w_ref[OFFSETS - 1 - o].T


def flip(weights):
    return pl.pallas_call(
        flip_kernel,
        out_shape=pltpu.VMEM((OFFSETS * CH, CH), BF16),
        in_specs=[VMEM],
        out_specs=VMEM,
        compiler_params=pltpu.CompilerParams(vmem_limit_bytes=8 << 20),
        cost_estimate=pl.CostEstimate(flops=0, bytes_accessed=2 << 20, transcendentals=0),
        name="flip",
    )(weights)


def conv_kernel(first, pos_ref, occ_ref, patch_ref, rim_ref, w_ref, *rest):
    out_ref, acc = rest[-2:]
    s = first + pl.program_id(0)
    row = pos_ref[...].astype(F32)
    slot = lax.broadcasted_iota(jnp.int32, row.shape, 1)
    pos = jnp.sum(jnp.where(slot == s, row, 0.0)).astype(jnp.int32)

    @pl.when(pos >= 0)
    def _():
        columns = mask_columns(occ_ref)
        total = jnp.dot(patch_rows(patch_ref, s, 0), w_ref[:KROW], preferred_element_type=F32)
        for p in range(1, 3):
            total += jnp.dot(patch_rows(patch_ref, s, p), w_ref[p * KROW : (p + 1) * KROW], preferred_element_type=F32)
        acc[...] = total
        if rim_ref is not None:
            for end, edge in ((0, 0), (1, 3)):

                @pl.when((pos >> 2) == edge)
                def _():
                    rows = jnp.concatenate([rim_ref[s, pl.ds(q * 8, 64)] for q in range(3)], axis=1)
                    row, k = end * (VOX - 64), 2 * end * KROW
                    acc[row : row + 64] += jnp.dot(rows, w_ref[k : k + KROW], preferred_element_type=F32)

        lane = lax.broadcasted_iota(jnp.int32, columns.shape, 1)
        keep = jnp.sum(jnp.where(lane == s, columns, 0.0), axis=1, keepdims=True)
        out_ref[0] = jnp.where(jnp.broadcast_to(keep, (VOX, CH)) > 0.5, acc[...], 0.0).astype(BF16)

    @pl.when(pos < 0)
    def _():
        out_ref[0] = jnp.zeros((VOX, CH), BF16)


def convolve(slot_pos, occupancy, patch, rim, weights, out, first, count):
    given = [pin(slot_pos, pltpu.VMEM), pin(occupancy, pltpu.VMEM), pin(patch, pltpu.VMEM)] + ([] if rim is None else [pin(rim, pltpu.VMEM)]) + [pin(weights, pltpu.VMEM)]
    specs = [VMEM] * len(given)
    aliased = {}
    if out is not None:
        aliased = {len(given): 0}
        given.append(pin(out, pltpu.HBM))
        specs.append(HBM)

    def kernel(*refs):
        refs = list(refs)
        if rim is None:
            refs.insert(3, None)
        conv_kernel(first, *refs)

    return pl.pallas_call(
        kernel,
        out_shape=pltpu.HBM((SLOTS, VOX, CH), BF16),
        grid=(count,),
        in_specs=specs,
        out_specs=pl.BlockSpec((1, VOX, CH), lambda i: (first + i, 0, 0)),
        input_output_aliases=aliased,
        scratch_shapes=[pltpu.VMEM((VOX, CH), F32)],
        compiler_params=pltpu.CompilerParams(vmem_limit_bytes=12 << 20),
        cost_estimate=pl.CostEstimate(flops=count * 4 * VOX * OFFSETS * CH * CH, bytes_accessed=count << 20, transcendentals=0),
        name="convolve",
    )(*given)


def finish_kernel(mine, meta_ref, half_ref, *rest):
    out_hbm, rows, sems = rest[-3:]
    core = meta_ref[0]
    base = (core if mine else 1 - core) * BLOCKS
    order = meta_ref[1] if mine else meta_ref[2]
    scale = 1.0 / math.sqrt(float(256 * SLOTS * VOX))
    full = OFFSETS * CH // BROWS
    left = OFFSETS * CH - full * BROWS

    def copy(j, n):
        at = pl.multiple_of((base + (j ^ order)) * BROWS, 8)
        return pltpu.make_async_copy(rows.at[j, pl.ds(0, n)], out_hbm.at[pl.ds(at, n)], sems.at[j])

    def each(act):
        for j in range(BLOCKS):
            block = base + (j ^ order)

            @pl.when(block < full)
            def _():
                act(j, BROWS)

            @pl.when(block == full)
            def _():
                act(j, left)

    for j in range(BLOCKS):
        rows[j] = half_ref[j] * scale
    each(lambda j, n: copy(j, n).start())
    each(lambda j, n: copy(j, n).wait())


def finish(meta, half, out):
    given, specs = [meta, half], [SMEM, VMEM]
    if out is not None:
        given.append(pin(out, pltpu.HBM))
        specs.append(HBM)
    return pl.pallas_call(
        lambda *refs: finish_kernel(out is None, *refs),
        out_shape=pltpu.HBM((OFFSETS * CH, CH), F32),
        in_specs=specs,
        out_specs=HBM,
        input_output_aliases={} if out is None else {2: 0},
        scratch_shapes=[pltpu.VMEM((BLOCKS, BROWS, CH), F32), pltpu.SemaphoreType.DMA((BLOCKS,))],
        compiler_params=pltpu.CompilerParams(vmem_limit_bytes=8 << 20),
        cost_estimate=pl.CostEstimate(flops=0, bytes_accessed=2 << 20, transcendentals=0),
        name="finish",
    )(*given)


def make_shards(sizes):
    everyone = list(itertools.product(*[range(n) for n in sizes]))
    n_y_lo, n_core = sizes[3], sizes[4]
    narrow = n_y_lo * n_core
    wide = len(everyone) // narrow

    def number(at):
        flat = 0
        for a, n in zip(at, sizes):
            flat = flat * n + a
        return flat

    def mate(at, axis, k):
        y_hi, z, x, y_lo, core = at
        if isinstance(axis, tuple):
            axis = axis[core]
        y = y_hi * n_y_lo + y_lo
        if axis == "core":
            core ^= k
        elif axis == "x":
            x ^= k
        elif axis == "y":
            y ^= k
        else:
            z ^= k
        return (y // n_y_lo, z, x, y % n_y_lo, core)

    def swap(value, axis, k):
        return lax.ppermute(value, AXES, [(number(a), number(mate(a, axis, k))) for a in everyone])

    def exchange_wide(value, start):
        pairs = [(i * narrow + j, k * narrow + j) for a in range(start, wide - 1, 2) for i, k in ((a, a + 1), (a + 1, a)) for j in range(narrow)]
        return lax.ppermute(value, AXES, pairs)

    def exchange_narrow(value, start):
        pairs = [(i * narrow + j, i * narrow + k) for i in range(wide) for a in range(start, narrow - 1, 2) for j, k in ((a, a + 1), (a + 1, a))]
        return lax.ppermute(value, AXES, pairs)

    first, second = ("y", "x"), ("x", "y")

    def tie(*values):
        return lax.optimization_barrier(values)

    def scatter(value, axis):
        n = value.shape[0] // 4
        return [swap(value[k * n : (k + 1) * n], axis, k) for k in (2, 1, 3)]

    def add(value, parts):
        total = value[: parts[0].shape[0]]
        for part in parts:
            total = total + part
        return total

    def copies(value, axis, ks):
        return [swap(value, axis, k) for k in ks]

    def join(value, parts):
        return jnp.concatenate([value, parts[1], parts[0], parts[2]], axis=0)

    def shards(features, weights, cotangent, occupancy, slot_pos):
        slot_row = slot_pos.reshape(1, SLOTS)
        slot_pos = pin(slot_pos, pltpu.HBM)
        core = lax.axis_index("core")
        x_at = lax.axis_index("x")
        y_at = lax.axis_index("y_hi") * n_y_lo + lax.axis_index("y_lo")
        yx, xy = y_at * 4 + x_at, x_at * 4 + y_at
        odd_x = x_at & 1
        meta = jnp.stack([core, jnp.where(core == 0, yx, xy), jnp.where(core == 0, xy, yx), odd_x]).astype(jnp.int32)
        xt, even, odd, side_even, side_odd = place(slot_pos, meta, occupancy, features, cotangent)
        side_even, side_odd, source = tie(side_even, side_odd, weights)
        side_even = exchange_narrow(side_even, 0)
        side_odd = exchange_narrow(side_odd, 1)
        side_even, side_odd, w_backward = tie(side_even, side_odd, flip(source))

        def rim(plane, last):
            ends = [jnp.where(last, v[:, NX - 1 :], v[:, :1]) for v in (side_even, side_odd)]
            first = core == 0
            return jnp.concatenate([jnp.where(first, ends[1], ends[0]), plane, jnp.where(first, ends[0], ends[1])], axis=1)

        even, odd = rim(even, odd_x == 0), rim(odd, odd_x == 1)
        even, odd, pos = tie(even, odd, slot_pos)
        even = exchange_wide(even, 0)
        odd = exchange_wide(odd, 1)
        cot_patch, total = weight_gradient(pos, meta, occupancy, cotangent, (side_even, side_odd), xt)
        even, odd, total = tie(even, odd, total)
        cot_rim, keep, send = rim_terms(slot_pos, meta, (even, odd), xt, total)
        w_forward = weights.reshape(OFFSETS * CH, CH)
        done = {"outputs": None, "grad_input": None, "patch": None}

        def backward(at, row):
            done["grad_input"] = convolve(row, occupancy, cot_patch, cot_rim, w_backward, done["grad_input"], *at)
            return "grad_input"

        def forward(at, row):
            done["outputs"] = convolve(row, occupancy, done["patch"], None, w_forward, done["outputs"], *at)
            return "outputs"

        def gather_patches(at, pos):
            done["patch"] = patches(pos, meta, occupancy, features, (side_even, side_odd), (even, odd))
            return "patch"

        def stage(value, start, *work):
            value, pos, row = tie(value, slot_pos, slot_row)
            parts = start(value)
            names = {call(at, pos if at is None else row) for call, at in work}
            held = tie(parts, *[done[n] for n in sorted(names)])
            for n, v in zip(sorted(names), held[1:]):
                done[n] = v
            return value, held[0]

        _, (got,) = stage(send, lambda v: copies(v, "core", (1,)), (backward, (0, 1)))
        total = keep + got
        total = add(*stage(total, lambda v: scatter(v, first), (backward, (1, 4))))
        total = add(*stage(total, lambda v: scatter(v, second), (backward, (5, 2))))
        total = add(*stage(total, lambda v: copies(v, "z", (2, 1, 3)), (gather_patches, None)))
        total = add(*stage(total, lambda v: copies(v, "z", (4,)), (backward, (7, 1)), (forward, (0, 1))))
        total = join(*stage(total, lambda v: copies(v, second, (2, 1, 3)), (forward, (1, 2))))
        total = join(*stage(total, lambda v: copies(v, first, (2, 1, 3)), (forward, (3, 4))))

        def finish_own(at, pos):
            done["grad_weight"] = finish(meta, total, None)
            return "grad_weight"

        total, (got,) = stage(total, lambda v: copies(v, "core", (1,)), (finish_own, None), (forward, (7, 1)))
        grad_weight = finish(meta, got, done["grad_weight"]).reshape(OFFSETS, CH, CH)
        return done["outputs"], done["grad_input"], grad_weight

    return shards


def solution(mesh):
    sizes = (2, 8, 4, 2, 2)
    fine = Mesh(mesh.devices.reshape(sizes), AXES)
    return jax.shard_map(
        make_shards(sizes),
        mesh=fine,
        in_specs=(P(AXES, None, None), P(), P(AXES, None, None), P(AXES, None), P(AXES)),
        out_specs=(P(AXES, None, None), P(AXES, None, None), P()),
        check_vma=False,
    )
```

profile of v0, /device:TPU:1, one launch (start us, length us, event | category | flops | bytes accessed | tf_op | source)
XLA Modules:
  0.0 101.7 jit_solution(17952764255720630256)
XLA Ops:
  0.7 4.2 %place.1 = (bf16[8,128,512]{2,1,0:T(8,128)(2,1)S(1)}, bf16[2,16,16,128]{3,2,1,0:T(8,128)(2,1)S(1)}, bf16[2,16,16,128]{3,2,1,0:T(8,128)(2,1)S(1)}, bf16[2,32,16,1...) custom-call(s32[8]{0:T(128)} %pos_ref.5, s32[4]{0:T(128)S(1)} %pad_add_fusion.meta_ref.refs_0_, s32[8,512]{1,0:T(8,128)} %refs_1_.15, ...), custom_call_target="tpu_custom_call" | custom-call | tf_op jit(solution)/shard_map/place/pallas_call | solution.py:116
  5.0 4.3 %collective-permute-start = (bf16[2,32,16,128]{3,2,1,0:T(8,128)(2,1)S(1)}, bf16[2,32,16,128]{3,2,1,0:T(8,128)(2,1)S(1)}, u32[]{:S(2)}, u32[]{:S(2)}) collective-permute-start(bf16[2,32,16,128]{3,2,1,0:T(8,128)(2,1)S(1)} %get-tuple-element.71), channel_id=1, source_target_pairs={{0,1},{1,0},{2,3},{3,2},{4,5},{5,4},{6,7},{7,6},{8,9},{9,8},{10,11... | collective-permute-start | bytes 786440 | tf_op jit(solution)/shard_map/ppermute | solution.py:474
  9.3 1.9 %collective-permute-start.1 = (bf16[2,32,16,128]{3,2,1,0:T(8,128)(2,1)S(1)}, bf16[2,32,16,128]{3,2,1,0:T(8,128)(2,1)S(1)}, u32[]{:S(2)}, u32[]{:S(2)}) collective-permute-start(bf16[2,32,16,128]{3,2,1,0:T(8,128)(2,1)S(1)} %get-tuple-element.72), channel_id=1, source_target_pairs={{1,2},{2,1},{5,6},{6,5},{9,10},{10,9},{13,14},{14,13},{17,18},{18,... | collective-permute-start | bytes 786440 | tf_op jit(solution)/shard_map/ppermute | solution.py:474
  11.5 5.4 %collective-permute-done.1.side_odd_ref = bf16[2,32,16,128]{3,2,1,0:T(8,128)(2,1)S(1)} collective-permute-done((bf16[2,32,16,128]{3,2,1,0:T(8,128)(2,1)S(1)}, bf16[2,32,16,128]{3,2,1,0:T(8,128)(2,1)S(1)}, u32[]{:S(2)}, u32[]{:S(2)}) %collective-permute-start.1) | collective-permute-done | bytes 262176 | tf_op jit(solution)/shard_map/ppermute | solution.py:474
  17.1 0.7 collective-permute-start.3
  17.8 8.3 %weight_gradient.1 = (bf16[8,10,80,384]{3,2,1,0:T(8,128)(2,1)S(1)}, f32[3584,128]{1,0:T(8,128)S(1)}) custom-call(s32[8]{0:T(128)} %pos_ref.5, s32[4]{0:T(128)S(1)} %pad_add_fusion.meta_ref.refs_0_, s32[8,512]{1,0:T(8,128)} %refs_1_.15, bf16[8,512,128]{2,1,0:T(8,128)(2,1)} %slots_hbm.2, bf16[2,32,16,128]{3,2,1,0:T(8,128)(2,1)S(1)} %collective-permute-done.side_even_ref, ...), custom_call_target="tpu_custom_call" | custom-call | flops 3623878656 | bytes 20971520 | tf_op jit(solution)/shard_map/weight_gradient/pallas_call | solution.py:285
  26.2 2.2 %rim_terms.1 = (bf16[8,80,384]{2,1,0:T(8,128)(2,1)S(1)}, f32[16,112,128]{2,1,0:T(8,128)S(1)}, f32[16,112,128]{2,1,0:T(8,128)S(1)}) custom-call(s32[8]{0:T(128)} %pos_ref.5, s32[4]{0:T(128)S(1)} %pad_add_fusion.meta_ref.refs_0_, bf16[2,18,16,128]{3,2,1,0:T(8,128)(2,1)S(1)} %collective-permute-done.2.even_ref, ...), custom_call_target="tpu_custom_call" | custom-call | tf_op jit(solution)/shard_map/rim_terms/pallas_call | solution.py:300
  28.5 2.0 %convolve.8.refs_5_ = bf16[8,512,128]{2,1,0:T(8,128)(2,1)} custom-call(s32[1,8]{1,0:T(1,128)S(1)} %bitcast.11, s32[8,512]{1,0:T(8,128)S(1)} %copy-done.1, bf16[8,10,80,384]{3,2,1,0:T(8,128)(2,1)S(1)} %get-tuple-element.90.refs_2_, bf16[8,80,384]{2,1,0:T(8,128)(2,1)S(1)} %get-tuple-element.91.refs_3_, bf16[3456,128]{1,0:T(8,128)(2,1)S(1)} %flip.1.refs_4_), custom_call_target="tpu_custom_call" | custom-call | flops 905969664 | bytes 1048576 | tf_op jit(solution)/shard_map/convolve/pallas_call | solution.py:375
  31.1 5.6 %collective-permute-start.7 = (f32[4,112,128]{2,1,0:T(8,128)S(1)}, f32[4,112,128]{2,1,0:T(8,128)S(1)}, u32[]{:S(2)}, u32[]{:S(2)}) collective-permute-start(f32[4,112,128]{2,1,0:T(8,128)S(1)} %get-tuple-element.135), channel_id=1, source_target_pairs={{0,130},{1,13},{2,128},{3,15},{4,134},{5,9},{6,132},{7,11},{8,138}... | collective-permute-start | bytes 688136 | tf_op jit(solution)/shard_map/ppermute | solution.py:466
  36.7 1.3 %collective-permute-start.5 = (f32[4,112,128]{2,1,0:T(8,128)S(1)}, f32[4,112,128]{2,1,0:T(8,128)S(1)}, u32[]{:S(2)}, u32[]{:S(2)}) collective-permute-start(f32[4,112,128]{2,1,0:T(8,128)S(1)} %get-tuple-element.137), channel_id=1, source_target_pairs={{0,128},{1,9},{2,130},{3,11},{4,132},{5,13},{6,134},{7,15},{8,136}... | collective-permute-start | bytes 688136 | tf_op jit(solution)/shard_map/ppermute | solution.py:466
  38.0 6.9 %convolve.9.refs_5_ = bf16[8,512,128]{2,1,0:T(8,128)(2,1)} custom-call(s32[1,8]{1,0:T(1,128)S(1)} %bitcast.12, s32[8,512]{1,0:T(8,128)S(1)} %copy-done.1, bf16[8,10,80,384]{3,2,1,0:T(8,128)(2,1)S(1)} %get-tuple-element.90.refs_2_, bf16[8,80,384]{2,1,0:T(8,128)(2,1)S(1)} %get-tuple-element.91.refs_3_, ...), custom_call_target="tpu_custom_call", output_to_operand_aliasing={{}: (5, {})} | custom-call | flops 3623878656 | bytes 4194304 | tf_op jit(solution)/shard_map/convolve/pallas_call | solution.py:375
  45.0 8.3 %collective-permute-start.10 = (f32[1,112,128]{2,1,0:T(8,128)S(1)}, f32[1,112,128]{2,1,0:T(8,128)S(1)}, u32[]{:S(2)}, u32[]{:S(2)}) collective-permute-start(f32[1,112,128]{2,1,0:T(8,128)S(1)} %get-tuple-element.142), channel_id=1, source_target_pairs={{0,12},{1,131},{2,14},{3,129},{4,8},{5,135},{6,10},{7,133},{8,4},{... | collective-permute-start | bytes 172040 | tf_op jit(solution)/shard_map/ppermute | solution.py:466
  54.6 1.0 convolve.10.refs_5_
  55.6 1.0 %collective-permute-done.9 = f32[1,112,128]{2,1,0:T(8,128)S(1)} collective-permute-done((f32[1,112,128]{2,1,0:T(8,128)S(1)}, f32[1,112,128]{2,1,0:T(8,128)S(1)}, u32[]{:S(2)}, u32[]{:S(2)}) %collective-permute-start.9) | collective-permute-done | bytes 57376 | tf_op jit(solution)/shard_map/ppermute | solution.py:466
  56.6 2.1 %collective-permute-done.8 = f32[1,112,128]{2,1,0:T(8,128)S(1)} collective-permute-done((f32[1,112,128]{2,1,0:T(8,128)S(1)}, f32[1,112,128]{2,1,0:T(8,128)S(1)}, u32[]{:S(2)}, u32[]{:S(2)}) %collective-permute-start.8) | collective-permute-done | bytes 57376 | tf_op jit(solution)/shard_map/ppermute | solution.py:466
  58.9 3.4 %collective-permute-start.11 = (f32[1,112,128]{2,1,0:T(8,128)S(1)}, f32[1,112,128]{2,1,0:T(8,128)S(1)}, u32[]{:S(2)}, u32[]{:S(2)}) collective-permute-start(f32[1,112,128]{2,1,0:T(8,128)S(1)} %add_add_fusion.2), channel_id=1, source_target_pairs={{0,32},{1,33},{2,34},{3,35},{4,36},{5,37},{6,38},{7,39},{8,40},{9,... | collective-permute-start | bytes 172040 | tf_op jit(solution)/shard_map/ppermute | solution.py:466
  62.3 4.7 %patches.1.refs_2_ = bf16[8,10,80,384]{3,2,1,0:T(8,128)(2,1)S(1)} custom-call(s32[8]{0:T(128)} %pos_ref.5, s32[4]{0:T(128)S(1)} %pad_add_fusion.meta_ref.refs_0_, s32[8,512]{1,0:T(8,128)} %refs_1_.15, bf16[8,512,128]{2,1,0:T(8,128)(2,1)} %slots_hbm.3, bf16[2,32,16,128]{3,2,1,0:T(8,128)(2,1)S(1)} %collective-permute-done.side_even_ref, ...), custom_call_target="tpu_custom_call" | custom-call | bytes 20971520 | tf_op jit(solution)/shard_map/patches/pallas_call | solution.py:271
  67.1 2.0 %collective-permute-start.14 = (f32[1,112,128]{2,1,0:T(8,128)S(1)}, f32[1,112,128]{2,1,0:T(8,128)S(1)}, u32[]{:S(2)}, u32[]{:S(2)}) collective-permute-start(f32[1,112,128]{2,1,0:T(8,128)S(1)} %add_add_fusion.1), channel_id=1, source_target_pairs={{0,64},{1,65},{2,66},{3,67},{4,68},{5,69},{6,70},{7,71},{8,72},{9,... | collective-permute-start | bytes 172040 | tf_op jit(solution)/shard_map/ppermute | solution.py:466
  69.1 0.8 convolve.11
  69.9 1.9 %convolve.12.refs_4_ = bf16[8,512,128]{2,1,0:T(8,128)(2,1)} custom-call(s32[1,8]{1,0:T(1,128)S(1)} %bitcast.15, s32[8,512]{1,0:T(8,128)S(1)} %copy-done.2, bf16[8,10,80,384]{3,2,1,0:T(8,128)(2,1)S(1)} %patches.1.refs_2_, bf16[3456,128]{1,0:T(8,128)(2,1)S(1)} %bitcast.7), custom_call_target="tpu_custom_call" | custom-call | flops 905969664 | bytes 1048576 | tf_op jit(solution)/shard_map/convolve/pallas_call | solution.py:375
  71.8 2.4 %collective-permute-done.14 = f32[1,112,128]{2,1,0:T(8,128)S(1)} collective-permute-done((f32[1,112,128]{2,1,0:T(8,128)S(1)}, f32[1,112,128]{2,1,0:T(8,128)S(1)}, u32[]{:S(2)}, u32[]{:S(2)}) %collective-permute-start.14) | collective-permute-done | bytes 57376 | tf_op jit(solution)/shard_map/ppermute | solution.py:466
  74.2 1.0 collective-permute-start.17
  75.2 1.3 %collective-permute-start.16 = (f32[1,112,128]{2,1,0:T(8,128)S(1)}, f32[1,112,128]{2,1,0:T(8,128)S(1)}, u32[]{:S(2)}, u32[]{:S(2)}) collective-permute-start(f32[1,112,128]{2,1,0:T(8,128)S(1)} %add.55), channel_id=1, source_target_pairs={{0,4},{1,3},{2,6},{3,1},{4,0},{5,7},{6,2},{7,5},{8,12},{9,11},{10,... | collective-permute-start | bytes 172040 | tf_op jit(solution)/shard_map/ppermute | solution.py:466
  76.4 1.7 %collective-permute-start.15 = (f32[1,112,128]{2,1,0:T(8,128)S(1)}, f32[1,112,128]{2,1,0:T(8,128)S(1)}, u32[]{:S(2)}, u32[]{:S(2)}) collective-permute-start(f32[1,112,128]{2,1,0:T(8,128)S(1)} %add.55), channel_id=1, source_target_pairs={{0,8},{1,129},{2,10},{3,131},{4,12},{5,133},{6,14},{7,135},{8,0},{... | collective-permute-start | bytes 172040 | tf_op jit(solution)/shard_map/ppermute | solution.py:466
  78.1 3.1 %convolve.13.refs_4_ = bf16[8,512,128]{2,1,0:T(8,128)(2,1)} custom-call(s32[1,8]{1,0:T(1,128)S(1)} %bitcast.16, s32[8,512]{1,0:T(8,128)S(1)} %copy-done.2, bf16[8,10,80,384]{3,2,1,0:T(8,128)(2,1)S(1)} %patches.1.refs_2_, bf16[3456,128]{1,0:T(8,128)(2,1)S(1)} %bitcast.8, bf16[8,512,128]{2,1,0:T(8,128)(2,1)} %convolve.12.refs_4_), custom_call_target="tpu_custom_call", output_to_operand_aliasing={{}: (4, {})} | custom-call | flops 1811939328 | bytes 2097152 | tf_op jit(solution)/shard_map/convolve/pallas_call | solution.py:375
  81.7 3.5 %collective-permute-start.18 = (f32[4,112,128]{2,1,0:T(8,128)S(1)}, f32[4,112,128]{2,1,0:T(8,128)S(1)}, u32[]{:S(2)}, u32[]{:S(2)}) collective-permute-start(f32[4,112,128]{2,1,0:T(8,128)S(1)} %pad_maximum_fusion), channel_id=1, source_target_pairs={{0,128},{1,9},{2,130},{3,11},{4,132},{5,13},{6,134},{7,15},{8,136}... | collective-permute-start | bytes 688136 | tf_op jit(solution)/shard_map/ppermute | solution.py:466
  85.2 3.9 %convolve.14.refs_4_ = bf16[8,512,128]{2,1,0:T(8,128)(2,1)} custom-call(s32[1,8]{1,0:T(1,128)S(1)} %bitcast.17, s32[8,512]{1,0:T(8,128)S(1)} %copy-done.2, bf16[8,10,80,384]{3,2,1,0:T(8,128)(2,1)S(1)} %patches.1.refs_2_, bf16[3456,128]{1,0:T(8,128)(2,1)S(1)} %bitcast.9, bf16[8,512,128]{2,1,0:T(8,128)(2,1)} %convolve.13.refs_4_), custom_call_target="tpu_custom_call", output_to_operand_aliasing={{}: (4, {})} | custom-call | flops 3623878656 | bytes 4194304 | tf_op jit(solution)/shard_map/convolve/pallas_call | solution.py:375
  89.2 1.9 %collective-permute-done.18 = f32[4,112,128]{2,1,0:T(8,128)S(1)} collective-permute-done((f32[4,112,128]{2,1,0:T(8,128)S(1)}, f32[4,112,128]{2,1,0:T(8,128)S(1)}, u32[]{:S(2)}, u32[]{:S(2)}) %collective-permute-start.18) | collective-permute-done | bytes 229408 | tf_op jit(solution)/shard_map/ppermute | solution.py:466
  91.2 6.2 %collective-permute-start.21 = (f32[16,112,128]{2,1,0:T(8,128)S(1)}, f32[16,112,128]{2,1,0:T(8,128)S(1)}, u32[]{:S(2)}, u32[]{:S(2)}) collective-permute-start(f32[16,112,128]{2,1,0:T(8,128)S(1)} %constant_dynamic-update-slice_fusion.refs_1_), channel_id=1, source_target_pairs={{0,1},{1,0},{2,3},{3,2},{4,5},{5,4},{6,7},{7,6},{8,9},{9,8},{10,11... | collective-permute-start | bytes 2752520 | tf_op jit(solution)/shard_map/ppermute | solution.py:466
  97.4 1.6 %finish.2.refs_2_ = f32[3456,128]{1,0:T(8,128)} custom-call(s32[4]{0:T(128)S(1)} %pad_add_fusion.meta_ref.refs_0_, f32[16,112,128]{2,1,0:T(8,128)S(1)} %constant_dynamic-update-slice_fusion.refs_1_), custom_call_target="tpu_custom_call" | custom-call | bytes 2097152 | tf_op jit(solution)/shard_map/finish/pallas_call | solution.py:425
  99.0 0.8 convolve.15
  99.8 1.6 %finish.3 = f32[3456,128]{1,0:T(8,128)} custom-call(s32[4]{0:T(128)S(1)} %pad_add_fusion.meta_ref.refs_0_, f32[16,112,128]{2,1,0:T(8,128)S(1)} %collective-permute-done.21.refs_1_, f32[3456,128]{1,0:T(8,128)} %finish.2.refs_2_), custom_call_target="tpu_custom_call", output_to_operand_aliasing={{}: (2, {})} | custom-call | bytes 2097152 | tf_op jit(solution)/shard_map/finish/pallas_call | solution.py:425
  (52 shorter events, 3.3 us)
Async XLA Ops:
  0.6 10.6 %copy-start = (bf16[27,128,128]{2,1,0:T(8,128)(2,1)S(1)}, bf16[27,128,128]{2,1,0:T(8,128)(2,1)}, u32[]{:S(2)}) copy-start(bf16[27,128,128]{2,1,0:T(8,128)(2,1)} %w_ref) | copy-start | bytes 2654212
  5.0 6.5 %collective-permute-start = (bf16[2,32,16,128]{3,2,1,0:T(8,128)(2,1)S(1)}, bf16[2,32,16,128]{3,2,1,0:T(8,128)(2,1)S(1)}, u32[]{:S(2)}, u32[]{:S(2)}) collective-permute-start(bf16[2,32,16,128]{3,2,1,0:T(8,128)(2,1)S(1)} %get-tuple-element.71), channel_id=1, source_target_pairs={{0,1},{1,0},{2,3},{3,2},{4,5},{5,4},{6,7},{7,6},{8,9},{9,8},{10,11... | collective-permute-start | bytes 786440 | tf_op jit(solution)/shard_map/ppermute | solution.py:474
  9.3 7.7 %collective-permute-start.1 = (bf16[2,32,16,128]{3,2,1,0:T(8,128)(2,1)S(1)}, bf16[2,32,16,128]{3,2,1,0:T(8,128)(2,1)S(1)}, u32[]{:S(2)}, u32[]{:S(2)}) collective-permute-start(bf16[2,32,16,128]{3,2,1,0:T(8,128)(2,1)S(1)} %get-tuple-element.72), channel_id=1, source_target_pairs={{1,2},{2,1},{5,6},{6,5},{9,10},{10,9},{13,14},{14,13},{17,18},{18,... | collective-permute-start | bytes 786440 | tf_op jit(solution)/shard_map/ppermute | solution.py:474
  17.0 9.2 %collective-permute-start.2 = (bf16[2,18,16,128]{3,2,1,0:T(8,128)(2,1)S(1)}, bf16[2,18,16,128]{3,2,1,0:T(8,128)(2,1)S(1)}, u32[]{:S(2)}, u32[]{:S(2)}) collective-permute-start(bf16[2,18,16,128]{3,2,1,0:T(8,128)(2,1)S(1)} %get-tuple-element.78), channel_id=1, source_target_pairs={{0,4},{1,5},{2,6},{3,7},{4,0},{5,1},{6,2},{7,3},{8,12},{9,13},{10,... | collective-permute-start | bytes 442376 | tf_op jit(solution)/shard_map/ppermute | solution.py:470
  17.1 9.1 %collective-permute-start.3 = (bf16[2,18,16,128]{3,2,1,0:T(8,128)(2,1)S(1)}, bf16[2,18,16,128]{3,2,1,0:T(8,128)(2,1)S(1)}, u32[]{:S(2)}, u32[]{:S(2)}) collective-permute-start(bf16[2,18,16,128]{3,2,1,0:T(8,128)(2,1)S(1)} %get-tuple-element.79), channel_id=1, source_target_pairs={{4,8},{5,9},{6,10},{7,11},{8,4},{9,5},{10,6},{11,7},{12,16},{13,17... | collective-permute-start | bytes 442376 | tf_op jit(solution)/shard_map/ppermute | solution.py:470
  26.1 2.3 %copy-start.1 = (s32[8,512]{1,0:T(8,128)S(1)}, s32[8,512]{1,0:T(8,128)}, u32[]{:S(2)}) copy-start(s32[8,512]{1,0:T(8,128)} %refs_1_.15) | copy-start | bytes 49156
  26.2 2.3 %copy-start.3 = (s32[8]{0:T(128)S(1)}, s32[8]{0:T(128)}, u32[]{:S(2)}) copy-start(s32[8]{0:T(128)} %pos_ref.5) | copy-start | bytes 100
  28.4 2.6 %collective-permute-start.4 = (f32[16,112,128]{2,1,0:T(8,128)S(1)}, f32[16,112,128]{2,1,0:T(8,128)S(1)}, u32[]{:S(2)}, u32[]{:S(2)}) collective-permute-start(f32[16,112,128]{2,1,0:T(8,128)S(1)} %get-tuple-element.88), channel_id=1, source_target_pairs={{0,1},{1,0},{2,3},{3,2},{4,5},{5,4},{6,7},{7,6},{8,9},{9,8},{10,11... | collective-permute-start | bytes 2752520 | tf_op jit(solution)/shard_map/ppermute | solution.py:466
  31.1 13.8 %collective-permute-start.7 = (f32[4,112,128]{2,1,0:T(8,128)S(1)}, f32[4,112,128]{2,1,0:T(8,128)S(1)}, u32[]{:S(2)}, u32[]{:S(2)}) collective-permute-start(f32[4,112,128]{2,1,0:T(8,128)S(1)} %get-tuple-element.135), channel_id=1, source_target_pairs={{0,130},{1,13},{2,128},{3,15},{4,134},{5,9},{6,132},{7,11},{8,138}... | collective-permute-start | bytes 688136 | tf_op jit(solution)/shard_map/ppermute | solution.py:466
  36.7 8.2 %collective-permute-start.6 = (f32[4,112,128]{2,1,0:T(8,128)S(1)}, f32[4,112,128]{2,1,0:T(8,128)S(1)}, u32[]{:S(2)}, u32[]{:S(2)}) collective-permute-start(f32[4,112,128]{2,1,0:T(8,128)S(1)} %get-tuple-element.136), channel_id=1, source_target_pairs={{0,2},{1,5},{2,0},{3,7},{4,6},{5,1},{6,4},{7,3},{8,10},{9,13},{10,... | collective-permute-start | bytes 688136 | tf_op jit(solution)/shard_map/ppermute | solution.py:466
  36.7 8.2 %collective-permute-start.5 = (f32[4,112,128]{2,1,0:T(8,128)S(1)}, f32[4,112,128]{2,1,0:T(8,128)S(1)}, u32[]{:S(2)}, u32[]{:S(2)}) collective-permute-start(f32[4,112,128]{2,1,0:T(8,128)S(1)} %get-tuple-element.137), channel_id=1, source_target_pairs={{0,128},{1,9},{2,130},{3,11},{4,132},{5,13},{6,134},{7,15},{8,136}... | collective-permute-start | bytes 688136 | tf_op jit(solution)/shard_map/ppermute | solution.py:466
  45.0 10.6 %collective-permute-start.10 = (f32[1,112,128]{2,1,0:T(8,128)S(1)}, f32[1,112,128]{2,1,0:T(8,128)S(1)}, u32[]{:S(2)}, u32[]{:S(2)}) collective-permute-start(f32[1,112,128]{2,1,0:T(8,128)S(1)} %get-tuple-element.142), channel_id=1, source_target_pairs={{0,12},{1,131},{2,14},{3,129},{4,8},{5,135},{6,10},{7,133},{8,4},{... | collective-permute-start | bytes 172040 | tf_op jit(solution)/shard_map/ppermute | solution.py:466
  53.3 3.3 %collective-permute-start.9 = (f32[1,112,128]{2,1,0:T(8,128)S(1)}, f32[1,112,128]{2,1,0:T(8,128)S(1)}, u32[]{:S(2)}, u32[]{:S(2)}) collective-permute-start(f32[1,112,128]{2,1,0:T(8,128)S(1)} %get-tuple-element.143), channel_id=1, source_target_pairs={{0,4},{1,3},{2,6},{3,1},{4,0},{5,7},{6,2},{7,5},{8,12},{9,11},{10,... | collective-permute-start | bytes 172040 | tf_op jit(solution)/shard_map/ppermute | solution.py:466
  54.0 4.7 %collective-permute-start.8 = (f32[1,112,128]{2,1,0:T(8,128)S(1)}, f32[1,112,128]{2,1,0:T(8,128)S(1)}, u32[]{:S(2)}, u32[]{:S(2)}) collective-permute-start(f32[1,112,128]{2,1,0:T(8,128)S(1)} %get-tuple-element.144), channel_id=1, source_target_pairs={{0,8},{1,129},{2,10},{3,131},{4,12},{5,133},{6,14},{7,135},{8,0},{... | collective-permute-start | bytes 172040 | tf_op jit(solution)/shard_map/ppermute | solution.py:466
  58.7 10.4 %copy-start.2 = (s32[8,512]{1,0:T(8,128)S(1)}, s32[8,512]{1,0:T(8,128)}, u32[]{:S(2)}) copy-start(s32[8,512]{1,0:T(8,128)} %refs_1_.15) | copy-start | bytes 49156
  58.7 10.4 %copy-start.4 = (s32[8]{0:T(128)S(1)}, s32[8]{0:T(128)}, u32[]{:S(2)}) copy-start(s32[8]{0:T(128)} %pos_ref.5) | copy-start | bytes 100
  58.7 8.4 %collective-permute-start.13 = (f32[1,112,128]{2,1,0:T(8,128)S(1)}, f32[1,112,128]{2,1,0:T(8,128)S(1)}, u32[]{:S(2)}, u32[]{:S(2)}) collective-permute-start(f32[1,112,128]{2,1,0:T(8,128)S(1)} %add_add_fusion.2), channel_id=1, source_target_pairs={{0,48},{1,49},{2,50},{3,51},{4,52},{5,53},{6,54},{7,55},{8,56},{9,... | collective-permute-start | bytes 172040 | tf_op jit(solution)/shard_map/ppermute | solution.py:466
  58.8 8.3 %collective-permute-start.12 = (f32[1,112,128]{2,1,0:T(8,128)S(1)}, f32[1,112,128]{2,1,0:T(8,128)S(1)}, u32[]{:S(2)}, u32[]{:S(2)}) collective-permute-start(f32[1,112,128]{2,1,0:T(8,128)S(1)} %add_add_fusion.2), channel_id=1, source_target_pairs={{0,16},{1,17},{2,18},{3,19},{4,20},{5,21},{6,22},{7,23},{8,24},{9,... | collective-permute-start | bytes 172040 | tf_op jit(solution)/shard_map/ppermute | solution.py:466
  58.9 8.2 %collective-permute-start.11 = (f32[1,112,128]{2,1,0:T(8,128)S(1)}, f32[1,112,128]{2,1,0:T(8,128)S(1)}, u32[]{:S(2)}, u32[]{:S(2)}) collective-permute-start(f32[1,112,128]{2,1,0:T(8,128)S(1)} %add_add_fusion.2), channel_id=1, source_target_pairs={{0,32},{1,33},{2,34},{3,35},{4,36},{5,37},{6,38},{7,39},{8,40},{9,... | collective-permute-start | bytes 172040 | tf_op jit(solution)/shard_map/ppermute | solution.py:466
  67.1 7.1 %collective-permute-start.14 = (f32[1,112,128]{2,1,0:T(8,128)S(1)}, f32[1,112,128]{2,1,0:T(8,128)S(1)}, u32[]{:S(2)}, u32[]{:S(2)}) collective-permute-start(f32[1,112,128]{2,1,0:T(8,128)S(1)} %add_add_fusion.1), channel_id=1, source_target_pairs={{0,64},{1,65},{2,66},{3,67},{4,68},{5,69},{6,70},{7,71},{8,72},{9,... | collective-permute-start | bytes 172040 | tf_op jit(solution)/shard_map/ppermute | solution.py:466
  74.2 7.1 %collective-permute-start.17 = (f32[1,112,128]{2,1,0:T(8,128)S(1)}, f32[1,112,128]{2,1,0:T(8,128)S(1)}, u32[]{:S(2)}, u32[]{:S(2)}) collective-permute-start(f32[1,112,128]{2,1,0:T(8,128)S(1)} %add.55), channel_id=1, source_target_pairs={{0,12},{1,131},{2,14},{3,129},{4,8},{5,135},{6,10},{7,133},{8,4},{... | collective-permute-start | bytes 172040 | tf_op jit(solution)/shard_map/ppermute | solution.py:466
  75.2 6.1 %collective-permute-start.16 = (f32[1,112,128]{2,1,0:T(8,128)S(1)}, f32[1,112,128]{2,1,0:T(8,128)S(1)}, u32[]{:S(2)}, u32[]{:S(2)}) collective-permute-start(f32[1,112,128]{2,1,0:T(8,128)S(1)} %add.55), channel_id=1, source_target_pairs={{0,4},{1,3},{2,6},{3,1},{4,0},{5,7},{6,2},{7,5},{8,12},{9,11},{10,... | collective-permute-start | bytes 172040 | tf_op jit(solution)/shard_map/ppermute | solution.py:466
  76.4 4.8 %collective-permute-start.15 = (f32[1,112,128]{2,1,0:T(8,128)S(1)}, f32[1,112,128]{2,1,0:T(8,128)S(1)}, u32[]{:S(2)}, u32[]{:S(2)}) collective-permute-start(f32[1,112,128]{2,1,0:T(8,128)S(1)} %add.55), channel_id=1, source_target_pairs={{0,8},{1,129},{2,10},{3,131},{4,12},{5,133},{6,14},{7,135},{8,0},{... | collective-permute-start | bytes 172040 | tf_op jit(solution)/shard_map/ppermute | solution.py:466
  81.3 7.9 %collective-permute-start.20 = (f32[4,112,128]{2,1,0:T(8,128)S(1)}, f32[4,112,128]{2,1,0:T(8,128)S(1)}, u32[]{:S(2)}, u32[]{:S(2)}) collective-permute-start(f32[4,112,128]{2,1,0:T(8,128)S(1)} %pad_maximum_fusion), channel_id=1, source_target_pairs={{0,130},{1,13},{2,128},{3,15},{4,134},{5,9},{6,132},{7,11},{8,138}... | collective-permute-start | bytes 688136 | tf_op jit(solution)/shard_map/ppermute | solution.py:466
  81.5 7.7 %collective-permute-start.19 = (f32[4,112,128]{2,1,0:T(8,128)S(1)}, f32[4,112,128]{2,1,0:T(8,128)S(1)}, u32[]{:S(2)}, u32[]{:S(2)}) collective-permute-start(f32[4,112,128]{2,1,0:T(8,128)S(1)} %pad_maximum_fusion), channel_id=1, source_target_pairs={{0,2},{1,5},{2,0},{3,7},{4,6},{5,1},{6,4},{7,3},{8,10},{9,13},{10,... | collective-permute-start | bytes 688136 | tf_op jit(solution)/shard_map/ppermute | solution.py:466
  81.7 9.4 %collective-permute-start.18 = (f32[4,112,128]{2,1,0:T(8,128)S(1)}, f32[4,112,128]{2,1,0:T(8,128)S(1)}, u32[]{:S(2)}, u32[]{:S(2)}) collective-permute-start(f32[4,112,128]{2,1,0:T(8,128)S(1)} %pad_maximum_fusion), channel_id=1, source_target_pairs={{0,128},{1,9},{2,130},{3,11},{4,132},{5,13},{6,134},{7,15},{8,136}... | collective-permute-start | bytes 688136 | tf_op jit(solution)/shard_map/ppermute | solution.py:466
  91.2 8.7 %collective-permute-start.21 = (f32[16,112,128]{2,1,0:T(8,128)S(1)}, f32[16,112,128]{2,1,0:T(8,128)S(1)}, u32[]{:S(2)}, u32[]{:S(2)}) collective-permute-start(f32[16,112,128]{2,1,0:T(8,128)S(1)} %constant_dynamic-update-slice_fusion.refs_1_), channel_id=1, source_target_pairs={{0,1},{1,0},{2,3},{3,2},{4,5},{5,4},{6,7},{7,6},{8,9},{9,8},{10,11... | collective-permute-start | bytes 2752520 | tf_op jit(solution)/shard_map/ppermute | solution.py:466
where the time goes:
time: 103 us; the launch traced here: 102 us
  Pallas kernels  43.4 us (42%)
  starting transfers between devices  43.3 us (42%)
  waiting for transfers between devices  13.3 us (13%)
  between operations  1.13 us (1%)
    ppermute x18, starting transfers between devices, swap(): lax.ppermute(value, AXES, [(number(a), number(mate(a, axis, k))) for a in...  36.3 us
    pallas_call x8, Pallas kernels, convolve(): pl.pallas_call(kernel, out_shape=pltpu.HBM((SLOTS, VOX, CH), BF16), grid=...  20.4 us
    pallas_call x1, Pallas kernels, weight_gradient(): pl.pallas_call(weight_kernel, out_shape=(PATCH_SHAPE, TOTAL), grid=(SLOTS...  8.34 us
    ppermute x18, waiting for transfers between devices, swap(): lax.ppermute(value, AXES, [(number(a), number(mate(a, axis, k))) for a in...  7.84 us
    ppermute x2, starting transfers between devices, exchange_narrow(): return lax.ppermute(value, AXES, pairs)  6.21 us
    ppermute x2, waiting for transfers between devices, exchange_narrow(): return lax.ppermute(value, AXES, pairs)  5.45 us
    pallas_call x1, Pallas kernels, patches(): pl.pallas_call(patches_kernel, out_shape=PATCH_SHAPE, grid=(SLOTS,), in_s...  4.72 us
    pallas_call x1, Pallas kernels, place(): pl.pallas_call(place_kernel, out_shape=(pltpu.VMEM((SLOTS, CH, VOX), BF16...  4.22 us
  transfers between devices with their start and end apart: 22, of which 6 were waited for; matrix products, arithmetic and copies ran while one was open for 0% of the time, Pallas kernels for 35%

commit v1 on v0

--- a/solution.py
+++ b/solution.py
@@ -139,7 +139,7 @@
     return [a.reshape(n, 2, 8, CH) for a in (back, flat, ahead)]
 
 
-def assemble(meta_ref, t, cells_ref, side_even_ref, side_odd_ref, halo, planes=None):
+def assemble(meta_ref, t, cells_ref, side_even_ref, side_odd_ref, halo, planes):
     core, odd_x = meta_ref[0], meta_ref[3]
 
     def body(x, carry):
@@ -153,12 +153,9 @@
             for bz in range(2):
                 halo[r, bz, pl.ds(1, NX), y] = a[:, bz]
     for i, x in enumerate(((NX + 1) * (1 - odd_x), (NX + 1) * odd_x)):
-        if planes is None:
-            halo[:, :, x] = jnp.zeros((3, 2, NY + 2, 8, CH), F32)
-        else:
-            for r, a in enumerate(shifted(planes[i][t])):
-                for bz in range(2):
-                    halo[r, bz, x] = a[:, bz]
+        for r, a in enumerate(shifted(planes[i][t])):
+            for bz in range(2):
+                halo[r, bz, x] = a[:, bz]
     lax.fori_loop(0, NX, body, 0)
 
 
@@ -190,13 +187,33 @@
         build_patches(s, pos, halo, patch_ref)
 
 
-def weight_kernel(pos_ref, meta_ref, occ_hbm, slots_hbm, side_even_ref, side_odd_ref, xt_ref, patch_ref, total, halo, cells, occ, slots, sems):
+def prepare_kernel(pos_ref, occ_hbm, slots_hbm, w_hbm, halo, flipped, cells, occ, slots, sems, weights, w_sem):
+    load = pltpu.make_async_copy(w_hbm, weights, w_sem)
+    load.start()
+    fill(pos_ref, occ_hbm, slots_hbm, cells, occ, slots, sems)
+
+    def body(x, carry):
+        for r, a in enumerate(shifted(cells[x].reshape(NY, NZ, CH))):
+            for bz in range(2):
+                halo[r, bz, x] = a[:, bz]
+        return carry
+
+    lax.fori_loop(0, NX, body, 0)
+    load.wait()
+    for o in range(OFFSETS):
+        flipped[o * CH : (o + 1) * CH] = weights[OFFSETS - 1 - o].T
+
+
+def weight_kernel(pos_ref, meta_ref, halo, side_even_ref, side_odd_ref, xt_ref, patch_ref, total, columns):
     s = pl.program_id(0)
 
     @pl.when(s == 0)
     def _():
-        fill(pos_ref, occ_hbm, slots_hbm, cells, occ, slots, sems)
-        assemble(meta_ref, 0, cells, side_even_ref, side_odd_ref, halo)
+        core = meta_ref[0]
+        for end, ref in ((1 - core, side_even_ref), (core, side_odd_ref)):
+            for r, a in enumerate(shifted(ref[0])):
+                for bz in range(2):
+                    columns[end, r, bz] = a[:, bz]
 
         def clear(o, carry):
             total[pl.ds(pl.multiple_of(o * CH, CH), CH)] = jnp.zeros((CH, CH), F32)
@@ -208,7 +225,25 @@
 
     @pl.when(pos >= 0)
     def _():
-        build_patches(s, pos, halo, patch_ref)
+        bx, by, bz = brick_of(pos)
+        inner = jnp.where(by == 0, 8, 7)
+        for x in range(10):
+            at = bx * 8 + x - 1
+            for r in range(3):
+                if x == 0 or x == 9:
+                    valid = (at >= 0) & (at < NX)
+                    near = jnp.clip(at, 0, NX - 1)
+                else:
+                    valid, near = None, at
+                rows = halo[r, bz, near, pl.ds(by * 8, 8)]
+                other = halo[r, bz, near, pl.ds(inner, 1)]
+                outer = columns[by, r, bz, pl.ds(near, 1)]
+                first = jnp.where(by == 0, outer, other)
+                last = jnp.where(by == 0, other, outer)
+                whole = jnp.concatenate([first, rows, last], axis=0)
+                if valid is not None:
+                    whole = jnp.where(valid, whole, 0.0)
+                patch_ref[s, x, :, r * CH : (r + 1) * CH] = whole.reshape(PROWS, CH).astype(BF16)
         for p in range(3):
             terms = jnp.dot(xt_ref[0], patch_rows(patch_ref, s, p), preferred_element_type=F32)
             for k in range(9):
@@ -281,18 +316,34 @@
     )(slot_pos, meta, pin(occupancy, pltpu.HBM), pin(slots, pltpu.HBM), *sides, *planes)
 
 
-def weight_gradient(slot_pos, meta, occupancy, slots, sides, xt):
+PREPARED = pltpu.VMEM((3, 2, NX, NY, 8, CH), F32)
+
+
+def prepare(slot_pos, occupancy, slots, weights):
+    return pl.pallas_call(
+        prepare_kernel,
+        out_shape=(PREPARED, pltpu.VMEM((OFFSETS * CH, CH), BF16)),
+        in_specs=[SMEM, HBM, HBM, HBM],
+        out_specs=(VMEM, VMEM),
+        scratch_shapes=FILL + [pltpu.VMEM((OFFSETS, CH, CH), BF16), pltpu.SemaphoreType.DMA],
+        compiler_params=pltpu.CompilerParams(vmem_limit_bytes=26 << 20),
+        cost_estimate=pl.CostEstimate(flops=0, bytes_accessed=8 << 20, transcendentals=0),
+        name="prepare",
+    )(slot_pos, *[pin(a, pltpu.HBM) for a in (occupancy, slots, weights)])
+
+
+def weight_gradient(slot_pos, meta, prepared, sides, xt):
     return pl.pallas_call(
         weight_kernel,
         out_shape=(PATCH_SHAPE, TOTAL),
         grid=(SLOTS,),
-        in_specs=[SMEM, SMEM, HBM, HBM] + [VMEM] * 2 + [pl.BlockSpec((1, CH, VOX), lambda s: (s, 0, 0))],
+        in_specs=[SMEM, SMEM] + [VMEM] * 3 + [pl.BlockSpec((1, CH, VOX), lambda s: (s, 0, 0))],
         out_specs=(VMEM, VMEM),
-        scratch_shapes=[HALO] + FILL,
+        scratch_shapes=[pltpu.VMEM((2, 3, 2, NX, 8, CH), F32)],
         compiler_params=pltpu.CompilerParams(vmem_limit_bytes=30 << 20),
         cost_estimate=pl.CostEstimate(flops=2 * 4096 * OFFSETS * CH * CH, bytes_accessed=20 << 20, transcendentals=0),
         name="weight_gradient",
-    )(slot_pos, meta, pin(occupancy, pltpu.HBM), pin(slots, pltpu.HBM), *sides, xt)
+    )(slot_pos, meta, pin(prepared, pltpu.VMEM), *sides, xt)
 
 
 def rim_terms(slot_pos, meta, planes, xt, total):
@@ -306,23 +357,6 @@
         compiler_params=pltpu.CompilerParams(vmem_limit_bytes=20 << 20),
         name="rim_terms",
     )(slot_pos, meta, *planes, xt, total)
-
-
-def flip_kernel(w_ref, out_ref):
-    for o in range(OFFSETS):
-        out_ref[o * CH : (o + 1) * CH] = w_ref[OFFSETS - 1 - o].T
-
-
-def flip(weights):
-    return pl.pallas_call(
-        flip_kernel,
-        out_shape=pltpu.VMEM((OFFSETS * CH, CH), BF16),
-        in_specs=[VMEM],
-        out_specs=VMEM,
-        compiler_params=pltpu.CompilerParams(vmem_limit_bytes=8 << 20),
-        cost_estimate=pl.CostEstimate(flops=0, bytes_accessed=2 << 20, transcendentals=0),
-        name="flip",
-    )(weights)
 
 
 def conv_kernel(first, pos_ref, occ_ref, patch_ref, rim_ref, w_ref, *rest):
@@ -504,10 +538,11 @@
         odd_x = x_at & 1
         meta = jnp.stack([core, jnp.where(core == 0, yx, xy), jnp.where(core == 0, xy, yx), odd_x]).astype(jnp.int32)
         xt, even, odd, side_even, side_odd = place(slot_pos, meta, occupancy, features, cotangent)
-        side_even, side_odd, source = tie(side_even, side_odd, weights)
+        side_even, side_odd, pos = tie(side_even, side_odd, slot_pos)
         side_even = exchange_narrow(side_even, 0)
         side_odd = exchange_narrow(side_odd, 1)
-        side_even, side_odd, w_backward = tie(side_even, side_odd, flip(source))
+        prepared, w_backward = prepare(pos, occupancy, cotangent, weights)
+        side_even, side_odd, w_backward = tie(side_even, side_odd, w_backward)
 
         def rim(plane, last):
             ends = [jnp.where(last, v[:, NX - 1 :], v[:, :1]) for v in (side_even, side_odd)]
@@ -518,7 +553,7 @@
         even, odd, pos = tie(even, odd, slot_pos)
         even = exchange_wide(even, 0)
         odd = exchange_wide(odd, 1)
-        cot_patch, total = weight_gradient(pos, meta, occupancy, cotangent, (side_even, side_odd), xt)
+        cot_patch, total = weight_gradient(pos, meta, prepared, (side_even, side_odd), xt)
         even, odd, total = tie(even, odd, total)
         cot_rim, keep, send = rim_terms(slot_pos, meta, (even, odd), xt, total)
         w_forward = weights.reshape(OFFSETS * CH, CH)
@@ -547,18 +582,18 @@
 
         _, (got,) = stage(send, lambda v: copies(v, "core", (1,)), (backward, (0, 1)))
         total = keep + got
-        total = add(*stage(total, lambda v: scatter(v, first), (backward, (1, 4))))
-        total = add(*stage(total, lambda v: scatter(v, second), (backward, (5, 2))))
+        total = add(*stage(total, lambda v: scatter(v, first), (backward, (1, 3))))
+        total = add(*stage(total, lambda v: scatter(v, second), (backward, (4, 3))))
         total = add(*stage(total, lambda v: copies(v, "z", (2, 1, 3)), (gather_patches, None)))
-        total = add(*stage(total, lambda v: copies(v, "z", (4,)), (backward, (7, 1)), (forward, (0, 1))))
-        total = join(*stage(total, lambda v: copies(v, second, (2, 1, 3)), (forward, (1, 2))))
-        total = join(*stage(total, lambda v: copies(v, first, (2, 1, 3)), (forward, (3, 4))))
+        total = add(*stage(total, lambda v: copies(v, "z", (4,)), (backward, (7, 1)), (forward, (0, 2))))
+        total = join(*stage(total, lambda v: copies(v, second, (2, 1, 3)), (forward, (2, 2))))
+        total = join(*stage(total, lambda v: copies(v, first, (2, 1, 3)), (forward, (4, 4))))
 
         def finish_own(at, pos):
             done["grad_weight"] = finish(meta, total, None)
             return "grad_weight"
 
-        total, (got,) = stage(total, lambda v: copies(v, "core", (1,)), (finish_own, None), (forward, (7, 1)))
+        total, (got,) = stage(total, lambda v: copies(v, "core", (1,)), (finish_own, None))
         grad_weight = finish(meta, got, done["grad_weight"]).reshape(OFFSETS, CH, CH)
         return done["outputs"], done["grad_input"], grad_weight
 

time: 103 us -> 98.7 us (0.958)
  waiting for transfers between devices: 13.3 us -> 4.65 us
  Pallas kernels: 43.4 us -> 48.4 us
    pallas_call x1, Pallas kernels: 0.29 us -> 4.79 us  [prepare(): pl.pallas_call(prepare_kernel, out_shape=(PREPARED, pltpu.VMEM((OFFSETS *...]
    ppermute x18, waiting for transfers between devices: 7.84 us -> 3.48 us  [swap(): lax.ppermute(value, AXES, [(number(a), number(mate(a, axis, k))) for a in...]
    ppermute x2, waiting for transfers between devices: 5.45 us -> 1.17 us  [exchange_narrow(): return lax.ppermute(value, AXES, pairs)]
    pallas_call x1, Pallas kernels: 8.34 us -> 6.04 us  [weight_gradient(): pl.pallas_call(weight_kernel, out_shape=(PATCH_SHAPE, TOTAL), grid=(SLOTS...]
    pallas_call x8 -> x7, Pallas kernels: 20.4 us -> 22.1 us  [convolve(): pl.pallas_call(kernel, out_shape=pltpu.HBM((SLOTS, VOX, CH), BF16), grid=...]
  transfers between devices with their start and end apart: 22 -> 22, of which waited for: 6 -> 6; matrix products, arithmetic and copies ran while one was open for 0% -> 0% of each run, Pallas kernels for 35% -> 40%
where the time goes in v1:
time: 98.7 us; the launch traced here: 98 us
  Pallas kernels  48.4 us (49%)
  starting transfers between devices  43.3 us (44%)
  waiting for transfers between devices  4.65 us (5%)
  between operations  1.1 us (1%)
    ppermute x18, starting transfers between devices, swap(): lax.ppermute(value, AXES, [(number(a), number(mate(a, axis, k))) for a in...  37.2 us
    pallas_call x7, Pallas kernels, convolve(): pl.pallas_call(kernel, out_shape=pltpu.HBM((SLOTS, VOX, CH), BF16), grid=...  22.1 us
    pallas_call x1, Pallas kernels, weight_gradient(): pl.pallas_call(weight_kernel, out_shape=(PATCH_SHAPE, TOTAL), grid=(SLOTS...  6.04 us
    ppermute x2, starting transfers between devices, exchange_narrow(): return lax.ppermute(value, AXES, pairs)  5.23 us
    pallas_call x1, Pallas kernels, place(): pl.pallas_call(place_kernel, out_shape=(pltpu.VMEM((SLOTS, CH, VOX), BF16...  5.2 us
    pallas_call x1, Pallas kernels, patches(): pl.pallas_call(patches_kernel, out_shape=PATCH_SHAPE, grid=(SLOTS,), in_s...  4.92 us
    pallas_call x1, Pallas kernels, prepare(): pl.pallas_call(prepare_kernel, out_shape=(PREPARED, pltpu.VMEM((OFFSETS *...  4.79 us
    ppermute x18, waiting for transfers between devices, swap(): lax.ppermute(value, AXES, [(number(a), number(mate(a, axis, k))) for a in...  3.48 us
  transfers between devices with their start and end apart: 22, of which 6 were waited for; matrix products, arithmetic and copies ran while one was open for 0% of the time, Pallas kernels for 40%

profile of v1, /device:TPU:1, one launch (start us, length us, event | category | flops | bytes accessed | tf_op | source)
XLA Modules:
  0.0 98.0 jit_solution(3439397487310586049)
XLA Ops:
  0.7 5.2 %place.1 = (bf16[8,128,512]{2,1,0:T(8,128)(2,1)S(1)}, bf16[2,16,16,128]{3,2,1,0:T(8,128)(2,1)S(1)}, bf16[2,16,16,128]{3,2,1,0:T(8,128)(2,1)S(1)}, bf16[2,32,16,1...) custom-call(s32[8]{0:T(128)} %pos_ref.6, s32[4]{0:T(128)S(1)} %pad_add_fusion.meta_ref.refs_0_, s32[8,512]{1,0:T(8,128)} %refs_1_.13, ...), custom_call_target="tpu_custom_call" | custom-call | tf_op jit(solution)/shard_map/place/pallas_call | solution.py:116
  5.9 3.3 %collective-permute-start = (bf16[2,32,16,128]{3,2,1,0:T(8,128)(2,1)}, bf16[2,32,16,128]{3,2,1,0:T(8,128)(2,1)S(1)}, u32[]{:S(2)}, u32[]{:S(2)}) collective-permute-start(bf16[2,32,16,128]{3,2,1,0:T(8,128)(2,1)} %get-tuple-element.71), channel_id=1, source_target_pairs={{0,1},{1,0},{2,3},{3,2},{4,5},{5,4},{6,7},{7,6},{8,9},{9,8},{10,11... | collective-permute-start | bytes 786440 | tf_op jit(solution)/shard_map/ppermute | solution.py:508
  9.3 1.9 %collective-permute-start.1 = (bf16[2,32,16,128]{3,2,1,0:T(8,128)(2,1)}, bf16[2,32,16,128]{3,2,1,0:T(8,128)(2,1)S(1)}, u32[]{:S(2)}, u32[]{:S(2)}) collective-permute-start(bf16[2,32,16,128]{3,2,1,0:T(8,128)(2,1)} %get-tuple-element.72), channel_id=1, source_target_pairs={{1,2},{2,1},{5,6},{6,5},{9,10},{10,9},{13,14},{14,13},{17,18},{18,... | collective-permute-start | bytes 786440 | tf_op jit(solution)/shard_map/ppermute | solution.py:508
  11.2 4.8 %prepare.1 = (f32[3,2,32,16,8,128]{5,4,3,2,1,0:T(8,128)S(1)}, bf16[3456,128]{1,0:T(8,128)(2,1)S(1)}) custom-call(s32[8]{0:T(128)} %pos_ref.6, s32[8,512]{1,0:T(8,128)} %refs_1_.13, bf16[8,512,128]{2,1,0:T(8,128)(2,1)} %slots_hbm.2, bf16[27,128,128]{2,1,0:T(8,128)(2,1)} %w_hbm.1), custom_call_target="tpu_custom_call" | custom-call | bytes 8388608 | tf_op jit(solution)/shard_map/prepare/pallas_call | solution.py:323
  16.0 1.2 %collective-permute-done.1.side_odd_ref = bf16[2,32,16,128]{3,2,1,0:T(8,128)(2,1)S(1)} collective-permute-done((bf16[2,32,16,128]{3,2,1,0:T(8,128)(2,1)}, bf16[2,32,16,128]{3,2,1,0:T(8,128)(2,1)S(1)}, u32[]{:S(2)}, u32[]{:S(2)}) %collective-permute-start.1) | collective-permute-done | bytes 262176 | tf_op jit(solution)/shard_map/ppermute | solution.py:508
  17.4 0.7 collective-permute-start.3
  18.1 6.0 %weight_gradient.1 = (bf16[8,10,80,384]{3,2,1,0:T(8,128)(2,1)S(1)}, f32[3584,128]{1,0:T(8,128)S(1)}) custom-call(s32[8]{0:T(128)} %pos_ref.6, s32[4]{0:T(128)S(1)} %pad_add_fusion.meta_ref.refs_0_, f32[3,2,32,16,8,128]{5,4,3,2,1,0:T(8,128)S(1)} %get-tuple-element.82.halo, bf16[2,32,16,128]{3,2,1,0:T(8,128)(2,1)S(1)} %collective-permute-done.side_even_ref, ...), custom_call_target="tpu_custom_call" | custom-call | flops 3623878656 | bytes 20971520 | tf_op jit(solution)/shard_map/weight_gradient/pallas_call | solution.py:336
  24.2 2.2 %rim_terms.1 = (bf16[8,80,384]{2,1,0:T(8,128)(2,1)S(1)}, f32[16,112,128]{2,1,0:T(8,128)S(1)}, f32[16,112,128]{2,1,0:T(8,128)S(1)}) custom-call(s32[8]{0:T(128)} %pos_ref.6, s32[4]{0:T(128)S(1)} %pad_add_fusion.meta_ref.refs_0_, bf16[2,18,16,128]{3,2,1,0:T(8,128)(2,1)S(1)} %collective-permute-done.2.even_ref, ...), custom_call_target="tpu_custom_call" | custom-call | tf_op jit(solution)/shard_map/rim_terms/pallas_call | solution.py:351
  26.5 2.0 %convolve.7.refs_5_ = bf16[8,512,128]{2,1,0:T(8,128)(2,1)} custom-call(s32[1,8]{1,0:T(1,128)S(1)} %bitcast.10, s32[8,512]{1,0:T(8,128)S(1)} %copy-done.1, bf16[8,10,80,384]{3,2,1,0:T(8,128)(2,1)S(1)} %get-tuple-element.92.refs_2_, bf16[8,80,384]{2,1,0:T(8,128)(2,1)S(1)} %get-tuple-element.93.refs_3_, bf16[3456,128]{1,0:T(8,128)(2,1)S(1)} %get-tuple-element.94.refs_4_), custom_call_target="tpu_custom_call" | custom-call | flops 905969664 | bytes 1048576 | tf_op jit(solution)/shard_map/convolve/pallas_call | solution.py:409
  29.1 3.1 %collective-permute-start.7 = (f32[4,112,128]{2,1,0:T(8,128)S(1)}, f32[4,112,128]{2,1,0:T(8,128)S(1)}, u32[]{:S(2)}, u32[]{:S(2)}) collective-permute-start(f32[4,112,128]{2,1,0:T(8,128)S(1)} %get-tuple-element.135), channel_id=1, source_target_pairs={{0,130},{1,13},{2,128},{3,15},{4,134},{5,9},{6,132},{7,11},{8,138}... | collective-permute-start | bytes 688136 | tf_op jit(solution)/shard_map/ppermute | solution.py:500
  32.2 0.6 collective-permute-start.6
  32.8 1.0 %collective-permute-start.5 = (f32[4,112,128]{2,1,0:T(8,128)S(1)}, f32[4,112,128]{2,1,0:T(8,128)S(1)}, u32[]{:S(2)}, u32[]{:S(2)}) collective-permute-start(f32[4,112,128]{2,1,0:T(8,128)S(1)} %get-tuple-element.137), channel_id=1, source_target_pairs={{0,128},{1,9},{2,130},{3,11},{4,132},{5,13},{6,134},{7,15},{8,136}... | collective-permute-start | bytes 688136 | tf_op jit(solution)/shard_map/ppermute | solution.py:500
  33.8 5.3 %convolve.8.refs_5_ = bf16[8,512,128]{2,1,0:T(8,128)(2,1)} custom-call(s32[1,8]{1,0:T(1,128)S(1)} %bitcast.11, s32[8,512]{1,0:T(8,128)S(1)} %copy-done.1, bf16[8,10,80,384]{3,2,1,0:T(8,128)(2,1)S(1)} %get-tuple-element.92.refs_2_, bf16[8,80,384]{2,1,0:T(8,128)(2,1)S(1)} %get-tuple-element.93.refs_3_, ...), custom_call_target="tpu_custom_call", output_to_operand_aliasing={{}: (5, {})} | custom-call | flops 2717908992 | bytes 3145728 | tf_op jit(solution)/shard_map/convolve/pallas_call | solution.py:409
  39.1 0.5 collective-permute-done.5
  39.7 10.1 %collective-permute-start.10 = (f32[1,112,128]{2,1,0:T(8,128)S(1)}, f32[1,112,128]{2,1,0:T(8,128)S(1)}, u32[]{:S(2)}, u32[]{:S(2)}) collective-permute-start(f32[1,112,128]{2,1,0:T(8,128)S(1)} %get-tuple-element.142), channel_id=1, source_target_pairs={{0,12},{1,131},{2,14},{3,129},{4,8},{5,135},{6,10},{7,133},{8,4},{... | collective-permute-start | bytes 172040 | tf_op jit(solution)/shard_map/ppermute | solution.py:500
  49.9 1.3 %collective-permute-start.8 = (f32[1,112,128]{2,1,0:T(8,128)S(1)}, f32[1,112,128]{2,1,0:T(8,128)S(1)}, u32[]{:S(2)}, u32[]{:S(2)}) collective-permute-start(f32[1,112,128]{2,1,0:T(8,128)S(1)} %get-tuple-element.144), channel_id=1, source_target_pairs={{0,8},{1,129},{2,10},{3,131},{4,12},{5,133},{6,14},{7,135},{8,0},{... | collective-permute-start | bytes 172040 | tf_op jit(solution)/shard_map/ppermute | solution.py:500
  51.1 3.7 %convolve.9.refs_5_ = bf16[8,512,128]{2,1,0:T(8,128)(2,1)} custom-call(s32[1,8]{1,0:T(1,128)S(1)} %bitcast.12, s32[8,512]{1,0:T(8,128)S(1)} %copy-done.1, bf16[8,10,80,384]{3,2,1,0:T(8,128)(2,1)S(1)} %get-tuple-element.92.refs_2_, bf16[8,80,384]{2,1,0:T(8,128)(2,1)S(1)} %get-tuple-element.93.refs_3_, ...), custom_call_target="tpu_custom_call", output_to_operand_aliasing={{}: (5, {})} | custom-call | flops 2717908992 | bytes 3145728 | tf_op jit(solution)/shard_map/convolve/pallas_call | solution.py:409
  55.1 3.4 %collective-permute-start.11 = (f32[1,112,128]{2,1,0:T(8,128)S(1)}, f32[1,112,128]{2,1,0:T(8,128)S(1)}, u32[]{:S(2)}, u32[]{:S(2)}) collective-permute-start(f32[1,112,128]{2,1,0:T(8,128)S(1)} %add_add_fusion.2), channel_id=1, source_target_pairs={{0,32},{1,33},{2,34},{3,35},{4,36},{5,37},{6,38},{7,39},{8,40},{9,... | collective-permute-start | bytes 172040 | tf_op jit(solution)/shard_map/ppermute | solution.py:500
  58.6 4.9 %patches.1.refs_2_ = bf16[8,10,80,384]{3,2,1,0:T(8,128)(2,1)S(1)} custom-call(s32[8]{0:T(128)} %pos_ref.6, s32[4]{0:T(128)S(1)} %pad_add_fusion.meta_ref.refs_0_, s32[8,512]{1,0:T(8,128)} %refs_1_.13, bf16[8,512,128]{2,1,0:T(8,128)(2,1)} %slots_hbm.3, bf16[2,32,16,128]{3,2,1,0:T(8,128)(2,1)S(1)} %collective-permute-done.side_even_ref, ...), custom_call_target="tpu_custom_call" | custom-call | bytes 20971520 | tf_op jit(solution)/shard_map/patches/pallas_call | solution.py:306
  63.5 4.3 %collective-permute-start.14 = (f32[1,112,128]{2,1,0:T(8,128)S(1)}, f32[1,112,128]{2,1,0:T(8,128)S(1)}, u32[]{:S(2)}, u32[]{:S(2)}) collective-permute-start(f32[1,112,128]{2,1,0:T(8,128)S(1)} %add_add_fusion.1), channel_id=1, source_target_pairs={{0,64},{1,65},{2,66},{3,67},{4,68},{5,69},{6,70},{7,71},{8,72},{9,... | collective-permute-start | bytes 172040 | tf_op jit(solution)/shard_map/ppermute | solution.py:500
  67.9 3.1 %convolve.11.refs_4_ = bf16[8,512,128]{2,1,0:T(8,128)(2,1)} custom-call(s32[1,8]{1,0:T(1,128)S(1)} %bitcast.13, s32[8,512]{1,0:T(8,128)S(1)} %copy-done.2, bf16[8,10,80,384]{3,2,1,0:T(8,128)(2,1)S(1)} %patches.1.refs_2_, bf16[3456,128]{1,0:T(8,128)(2,1)S(1)} %bitcast.7), custom_call_target="tpu_custom_call" | custom-call | flops 1811939328 | bytes 2097152 | tf_op jit(solution)/shard_map/convolve/pallas_call | solution.py:409
  71.0 0.8 convolve.10
  71.8 3.2 %collective-permute-start.17 = (f32[1,112,128]{2,1,0:T(8,128)S(1)}, f32[1,112,128]{2,1,0:T(8,128)S(1)}, u32[]{:S(2)}, u32[]{:S(2)}) collective-permute-start(f32[1,112,128]{2,1,0:T(8,128)S(1)} %add.55), channel_id=1, source_target_pairs={{0,12},{1,131},{2,14},{3,129},{4,8},{5,135},{6,10},{7,133},{8,4},{... | collective-permute-start | bytes 172040 | tf_op jit(solution)/shard_map/ppermute | solution.py:500
  75.0 1.3 %collective-permute-start.15 = (f32[1,112,128]{2,1,0:T(8,128)S(1)}, f32[1,112,128]{2,1,0:T(8,128)S(1)}, u32[]{:S(2)}, u32[]{:S(2)}) collective-permute-start(f32[1,112,128]{2,1,0:T(8,128)S(1)} %add.55), channel_id=1, source_target_pairs={{0,8},{1,129},{2,10},{3,131},{4,12},{5,133},{6,14},{7,135},{8,0},{... | collective-permute-start | bytes 172040 | tf_op jit(solution)/shard_map/ppermute | solution.py:500
  76.3 3.1 %convolve.12.refs_4_ = bf16[8,512,128]{2,1,0:T(8,128)(2,1)} custom-call(s32[1,8]{1,0:T(1,128)S(1)} %bitcast.15, s32[8,512]{1,0:T(8,128)S(1)} %copy-done.2, bf16[8,10,80,384]{3,2,1,0:T(8,128)(2,1)S(1)} %patches.1.refs_2_, bf16[3456,128]{1,0:T(8,128)(2,1)S(1)} %bitcast.8, bf16[8,512,128]{2,1,0:T(8,128)(2,1)} %convolve.11.refs_4_), custom_call_target="tpu_custom_call", output_to_operand_aliasing={{}: (4, {})} | custom-call | flops 1811939328 | bytes 2097152 | tf_op jit(solution)/shard_map/convolve/pallas_call | solution.py:409
  79.6 1.0 collective-permute-start.20
  80.6 3.0 %collective-permute-start.18 = (f32[4,112,128]{2,1,0:T(8,128)S(1)}, f32[4,112,128]{2,1,0:T(8,128)S(1)}, u32[]{:S(2)}, u32[]{:S(2)}) collective-permute-start(f32[4,112,128]{2,1,0:T(8,128)S(1)} %pad_maximum_fusion), channel_id=1, source_target_pairs={{0,128},{1,9},{2,130},{3,11},{4,132},{5,13},{6,134},{7,15},{8,136}... | collective-permute-start | bytes 688136 | tf_op jit(solution)/shard_map/ppermute | solution.py:500
  83.6 3.9 %convolve.13 = bf16[8,512,128]{2,1,0:T(8,128)(2,1)} custom-call(s32[1,8]{1,0:T(1,128)S(1)} %bitcast.16, s32[8,512]{1,0:T(8,128)S(1)} %copy-done.2, bf16[8,10,80,384]{3,2,1,0:T(8,128)(2,1)S(1)} %patches.1.refs_2_, bf16[3456,128]{1,0:T(8,128)(2,1)S(1)} %bitcast.9, bf16[8,512,128]{2,1,0:T(8,128)(2,1)} %convolve.12.refs_4_), custom_call_target="tpu_custom_call", output_to_operand_aliasing={{}: (4, {})} | custom-call | flops 3623878656 | bytes 4194304 | tf_op jit(solution)/shard_map/convolve/pallas_call | solution.py:409
  87.5 1.9 %collective-permute-done.18 = f32[4,112,128]{2,1,0:T(8,128)S(1)} collective-permute-done((f32[4,112,128]{2,1,0:T(8,128)S(1)}, f32[4,112,128]{2,1,0:T(8,128)S(1)}, u32[]{:S(2)}, u32[]{:S(2)}) %collective-permute-start.18) | collective-permute-done | bytes 229408 | tf_op jit(solution)/shard_map/ppermute | solution.py:500
  89.5 4.6 %collective-permute-start.21 = (f32[16,112,128]{2,1,0:T(8,128)S(1)}, f32[16,112,128]{2,1,0:T(8,128)S(1)}, u32[]{:S(2)}, u32[]{:S(2)}) collective-permute-start(f32[16,112,128]{2,1,0:T(8,128)S(1)} %constant_dynamic-update-slice_fusion.refs_1_), channel_id=1, source_target_pairs={{0,1},{1,0},{2,3},{3,2},{4,5},{5,4},{6,7},{7,6},{8,9},{9,8},{10,11... | collective-permute-start | bytes 2752520 | tf_op jit(solution)/shard_map/ppermute | solution.py:500
  94.1 1.6 %finish.2.refs_2_ = f32[3456,128]{1,0:T(8,128)} custom-call(s32[4]{0:T(128)S(1)} %pad_add_fusion.meta_ref.refs_0_, f32[16,112,128]{2,1,0:T(8,128)S(1)} %constant_dynamic-update-slice_fusion.refs_1_), custom_call_target="tpu_custom_call" | custom-call | bytes 2097152 | tf_op jit(solution)/shard_map/finish/pallas_call | solution.py:459
  96.2 1.6 %finish.3 = f32[3456,128]{1,0:T(8,128)} custom-call(s32[4]{0:T(128)S(1)} %pad_add_fusion.meta_ref.refs_0_, f32[16,112,128]{2,1,0:T(8,128)S(1)} %collective-permute-done.21.refs_1_, f32[3456,128]{1,0:T(8,128)} %finish.2.refs_2_), custom_call_target="tpu_custom_call", output_to_operand_aliasing={{}: (2, {})} | custom-call | bytes 2097152 | tf_op jit(solution)/shard_map/finish/pallas_call | solution.py:459
  (51 shorter events, 2.1 us)
Async XLA Ops:
  5.9 10.0 %collective-permute-start = (bf16[2,32,16,128]{3,2,1,0:T(8,128)(2,1)}, bf16[2,32,16,128]{3,2,1,0:T(8,128)(2,1)S(1)}, u32[]{:S(2)}, u32[]{:S(2)}) collective-permute-start(bf16[2,32,16,128]{3,2,1,0:T(8,128)(2,1)} %get-tuple-element.71), channel_id=1, source_target_pairs={{0,1},{1,0},{2,3},{3,2},{4,5},{5,4},{6,7},{7,6},{8,9},{9,8},{10,11... | collective-permute-start | bytes 786440 | tf_op jit(solution)/shard_map/ppermute | solution.py:508
  9.3 7.9 %collective-permute-start.1 = (bf16[2,32,16,128]{3,2,1,0:T(8,128)(2,1)}, bf16[2,32,16,128]{3,2,1,0:T(8,128)(2,1)S(1)}, u32[]{:S(2)}, u32[]{:S(2)}) collective-permute-start(bf16[2,32,16,128]{3,2,1,0:T(8,128)(2,1)} %get-tuple-element.72), channel_id=1, source_target_pairs={{1,2},{2,1},{5,6},{6,5},{9,10},{10,9},{13,14},{14,13},{17,18},{18,... | collective-permute-start | bytes 786440 | tf_op jit(solution)/shard_map/ppermute | solution.py:508
  17.2 7.0 %collective-permute-start.2 = (bf16[2,18,16,128]{3,2,1,0:T(8,128)(2,1)S(1)}, bf16[2,18,16,128]{3,2,1,0:T(8,128)(2,1)S(1)}, u32[]{:S(2)}, u32[]{:S(2)}) collective-permute-start(bf16[2,18,16,128]{3,2,1,0:T(8,128)(2,1)S(1)} %get-tuple-element.79), channel_id=1, source_target_pairs={{0,4},{1,5},{2,6},{3,7},{4,0},{5,1},{6,2},{7,3},{8,12},{9,13},{10,... | collective-permute-start | bytes 442376 | tf_op jit(solution)/shard_map/ppermute | solution.py:504
  17.4 6.8 %collective-permute-start.3 = (bf16[2,18,16,128]{3,2,1,0:T(8,128)(2,1)S(1)}, bf16[2,18,16,128]{3,2,1,0:T(8,128)(2,1)S(1)}, u32[]{:S(2)}, u32[]{:S(2)}) collective-permute-start(bf16[2,18,16,128]{3,2,1,0:T(8,128)(2,1)S(1)} %get-tuple-element.80), channel_id=1, source_target_pairs={{4,8},{5,9},{6,10},{7,11},{8,4},{9,5},{10,6},{11,7},{12,16},{13,17... | collective-permute-start | bytes 442376 | tf_op jit(solution)/shard_map/ppermute | solution.py:504
  18.1 8.4 %copy-start.1 = (s32[8,512]{1,0:T(8,128)S(1)}, s32[8,512]{1,0:T(8,128)}, u32[]{:S(2)}) copy-start(s32[8,512]{1,0:T(8,128)} %refs_1_.13) | copy-start | bytes 49156
  18.1 8.4 %copy-start.3 = (s32[8]{0:T(128)S(1)}, s32[8]{0:T(128)}, u32[]{:S(2)}) copy-start(s32[8]{0:T(128)} %pos_ref.6) | copy-start | bytes 100
  26.4 2.6 %collective-permute-start.4 = (f32[16,112,128]{2,1,0:T(8,128)S(1)}, f32[16,112,128]{2,1,0:T(8,128)S(1)}, u32[]{:S(2)}, u32[]{:S(2)}) collective-permute-start(f32[16,112,128]{2,1,0:T(8,128)S(1)} %get-tuple-element.90), channel_id=1, source_target_pairs={{0,1},{1,0},{2,3},{3,2},{4,5},{5,4},{6,7},{7,6},{8,9},{9,8},{10,11... | collective-permute-start | bytes 2752520 | tf_op jit(solution)/shard_map/ppermute | solution.py:500
  29.1 10.0 %collective-permute-start.7 = (f32[4,112,128]{2,1,0:T(8,128)S(1)}, f32[4,112,128]{2,1,0:T(8,128)S(1)}, u32[]{:S(2)}, u32[]{:S(2)}) collective-permute-start(f32[4,112,128]{2,1,0:T(8,128)S(1)} %get-tuple-element.135), channel_id=1, source_target_pairs={{0,130},{1,13},{2,128},{3,15},{4,134},{5,9},{6,132},{7,11},{8,138}... | collective-permute-start | bytes 688136 | tf_op jit(solution)/shard_map/ppermute | solution.py:500
  32.2 6.9 %collective-permute-start.6 = (f32[4,112,128]{2,1,0:T(8,128)S(1)}, f32[4,112,128]{2,1,0:T(8,128)S(1)}, u32[]{:S(2)}, u32[]{:S(2)}) collective-permute-start(f32[4,112,128]{2,1,0:T(8,128)S(1)} %get-tuple-element.136), channel_id=1, source_target_pairs={{0,2},{1,5},{2,0},{3,7},{4,6},{5,1},{6,4},{7,3},{8,10},{9,13},{10,... | collective-permute-start | bytes 688136 | tf_op jit(solution)/shard_map/ppermute | solution.py:500
  32.8 6.9 %collective-permute-start.5 = (f32[4,112,128]{2,1,0:T(8,128)S(1)}, f32[4,112,128]{2,1,0:T(8,128)S(1)}, u32[]{:S(2)}, u32[]{:S(2)}) collective-permute-start(f32[4,112,128]{2,1,0:T(8,128)S(1)} %get-tuple-element.137), channel_id=1, source_target_pairs={{0,128},{1,9},{2,130},{3,11},{4,132},{5,13},{6,134},{7,15},{8,136}... | collective-permute-start | bytes 688136 | tf_op jit(solution)/shard_map/ppermute | solution.py:500
  39.7 15.2 %collective-permute-start.10 = (f32[1,112,128]{2,1,0:T(8,128)S(1)}, f32[1,112,128]{2,1,0:T(8,128)S(1)}, u32[]{:S(2)}, u32[]{:S(2)}) collective-permute-start(f32[1,112,128]{2,1,0:T(8,128)S(1)} %get-tuple-element.142), channel_id=1, source_target_pairs={{0,12},{1,131},{2,14},{3,129},{4,8},{5,135},{6,10},{7,133},{8,4},{... | collective-permute-start | bytes 172040 | tf_op jit(solution)/shard_map/ppermute | solution.py:500
  49.8 5.0 %collective-permute-start.9 = (f32[1,112,128]{2,1,0:T(8,128)S(1)}, f32[1,112,128]{2,1,0:T(8,128)S(1)}, u32[]{:S(2)}, u32[]{:S(2)}) collective-permute-start(f32[1,112,128]{2,1,0:T(8,128)S(1)} %get-tuple-element.143), channel_id=1, source_target_pairs={{0,4},{1,3},{2,6},{3,1},{4,0},{5,7},{6,2},{7,5},{8,12},{9,11},{10,... | collective-permute-start | bytes 172040 | tf_op jit(solution)/shard_map/ppermute | solution.py:500
  49.9 5.0 %collective-permute-start.8 = (f32[1,112,128]{2,1,0:T(8,128)S(1)}, f32[1,112,128]{2,1,0:T(8,128)S(1)}, u32[]{:S(2)}, u32[]{:S(2)}) collective-permute-start(f32[1,112,128]{2,1,0:T(8,128)S(1)} %get-tuple-element.144), channel_id=1, source_target_pairs={{0,8},{1,129},{2,10},{3,131},{4,12},{5,133},{6,14},{7,135},{8,0},{... | collective-permute-start | bytes 172040 | tf_op jit(solution)/shard_map/ppermute | solution.py:500
  54.9 13.0 %copy-start = (bf16[27,128,128]{2,1,0:T(8,128)(2,1)S(1)}, bf16[27,128,128]{2,1,0:T(8,128)(2,1)}, u32[]{:S(2)}) copy-start(bf16[27,128,128]{2,1,0:T(8,128)(2,1)} %w_hbm.1) | copy-start | bytes 2654212
  54.9 13.0 %copy-start.2 = (s32[8,512]{1,0:T(8,128)S(1)}, s32[8,512]{1,0:T(8,128)}, u32[]{:S(2)}) copy-start(s32[8,512]{1,0:T(8,128)} %refs_1_.13) | copy-start | bytes 49156
  54.9 13.0 %copy-start.4 = (s32[8]{0:T(128)S(1)}, s32[8]{0:T(128)}, u32[]{:S(2)}) copy-start(s32[8]{0:T(128)} %pos_ref.6) | copy-start | bytes 100
  54.9 8.6 %collective-permute-start.13 = (f32[1,112,128]{2,1,0:T(8,128)S(1)}, f32[1,112,128]{2,1,0:T(8,128)S(1)}, u32[]{:S(2)}, u32[]{:S(2)}) collective-permute-start(f32[1,112,128]{2,1,0:T(8,128)S(1)} %add_add_fusion.2), channel_id=1, source_target_pairs={{0,48},{1,49},{2,50},{3,51},{4,52},{5,53},{6,54},{7,55},{8,56},{9,... | collective-permute-start | bytes 172040 | tf_op jit(solution)/shard_map/ppermute | solution.py:500
  55.1 8.5 %collective-permute-start.12 = (f32[1,112,128]{2,1,0:T(8,128)S(1)}, f32[1,112,128]{2,1,0:T(8,128)S(1)}, u32[]{:S(2)}, u32[]{:S(2)}) collective-permute-start(f32[1,112,128]{2,1,0:T(8,128)S(1)} %add_add_fusion.2), channel_id=1, source_target_pairs={{0,16},{1,17},{2,18},{3,19},{4,20},{5,21},{6,22},{7,23},{8,24},{9,... | collective-permute-start | bytes 172040 | tf_op jit(solution)/shard_map/ppermute | solution.py:500
  55.1 8.4 %collective-permute-start.11 = (f32[1,112,128]{2,1,0:T(8,128)S(1)}, f32[1,112,128]{2,1,0:T(8,128)S(1)}, u32[]{:S(2)}, u32[]{:S(2)}) collective-permute-start(f32[1,112,128]{2,1,0:T(8,128)S(1)} %add_add_fusion.2), channel_id=1, source_target_pairs={{0,32},{1,33},{2,34},{3,35},{4,36},{5,37},{6,38},{7,39},{8,40},{9,... | collective-permute-start | bytes 172040 | tf_op jit(solution)/shard_map/ppermute | solution.py:500
  63.5 8.3 %collective-permute-start.14 = (f32[1,112,128]{2,1,0:T(8,128)S(1)}, f32[1,112,128]{2,1,0:T(8,128)S(1)}, u32[]{:S(2)}, u32[]{:S(2)}) collective-permute-start(f32[1,112,128]{2,1,0:T(8,128)S(1)} %add_add_fusion.1), channel_id=1, source_target_pairs={{0,64},{1,65},{2,66},{3,67},{4,68},{5,69},{6,70},{7,71},{8,72},{9,... | collective-permute-start | bytes 172040 | tf_op jit(solution)/shard_map/ppermute | solution.py:500
  71.8 7.6 %collective-permute-start.17 = (f32[1,112,128]{2,1,0:T(8,128)S(1)}, f32[1,112,128]{2,1,0:T(8,128)S(1)}, u32[]{:S(2)}, u32[]{:S(2)}) collective-permute-start(f32[1,112,128]{2,1,0:T(8,128)S(1)} %add.55), channel_id=1, source_target_pairs={{0,12},{1,131},{2,14},{3,129},{4,8},{5,135},{6,10},{7,133},{8,4},{... | collective-permute-start | bytes 172040 | tf_op jit(solution)/shard_map/ppermute | solution.py:500
  75.0 4.4 %collective-permute-start.16 = (f32[1,112,128]{2,1,0:T(8,128)S(1)}, f32[1,112,128]{2,1,0:T(8,128)S(1)}, u32[]{:S(2)}, u32[]{:S(2)}) collective-permute-start(f32[1,112,128]{2,1,0:T(8,128)S(1)} %add.55), channel_id=1, source_target_pairs={{0,4},{1,3},{2,6},{3,1},{4,0},{5,7},{6,2},{7,5},{8,12},{9,11},{10,... | collective-permute-start | bytes 172040 | tf_op jit(solution)/shard_map/ppermute | solution.py:500
  75.0 4.5 %collective-permute-start.15 = (f32[1,112,128]{2,1,0:T(8,128)S(1)}, f32[1,112,128]{2,1,0:T(8,128)S(1)}, u32[]{:S(2)}, u32[]{:S(2)}) collective-permute-start(f32[1,112,128]{2,1,0:T(8,128)S(1)} %add.55), channel_id=1, source_target_pairs={{0,8},{1,129},{2,10},{3,131},{4,12},{5,133},{6,14},{7,135},{8,0},{... | collective-permute-start | bytes 172040 | tf_op jit(solution)/shard_map/ppermute | solution.py:500
  79.6 7.9 %collective-permute-start.20 = (f32[4,112,128]{2,1,0:T(8,128)S(1)}, f32[4,112,128]{2,1,0:T(8,128)S(1)}, u32[]{:S(2)}, u32[]{:S(2)}) collective-permute-start(f32[4,112,128]{2,1,0:T(8,128)S(1)} %pad_maximum_fusion), channel_id=1, source_target_pairs={{0,130},{1,13},{2,128},{3,15},{4,134},{5,9},{6,132},{7,11},{8,138}... | collective-permute-start | bytes 688136 | tf_op jit(solution)/shard_map/ppermute | solution.py:500
  80.6 6.9 %collective-permute-start.19 = (f32[4,112,128]{2,1,0:T(8,128)S(1)}, f32[4,112,128]{2,1,0:T(8,128)S(1)}, u32[]{:S(2)}, u32[]{:S(2)}) collective-permute-start(f32[4,112,128]{2,1,0:T(8,128)S(1)} %pad_maximum_fusion), channel_id=1, source_target_pairs={{0,2},{1,5},{2,0},{3,7},{4,6},{5,1},{6,4},{7,3},{8,10},{9,13},{10,... | collective-permute-start | bytes 688136 | tf_op jit(solution)/shard_map/ppermute | solution.py:500
  80.6 8.8 %collective-permute-start.18 = (f32[4,112,128]{2,1,0:T(8,128)S(1)}, f32[4,112,128]{2,1,0:T(8,128)S(1)}, u32[]{:S(2)}, u32[]{:S(2)}) collective-permute-start(f32[4,112,128]{2,1,0:T(8,128)S(1)} %pad_maximum_fusion), channel_id=1, source_target_pairs={{0,128},{1,9},{2,130},{3,11},{4,132},{5,13},{6,134},{7,15},{8,136}... | collective-permute-start | bytes 688136 | tf_op jit(solution)/shard_map/ppermute | solution.py:500
  89.5 6.7 %collective-permute-start.21 = (f32[16,112,128]{2,1,0:T(8,128)S(1)}, f32[16,112,128]{2,1,0:T(8,128)S(1)}, u32[]{:S(2)}, u32[]{:S(2)}) collective-permute-start(f32[16,112,128]{2,1,0:T(8,128)S(1)} %constant_dynamic-update-slice_fusion.refs_1_), channel_id=1, source_target_pairs={{0,1},{1,0},{2,3},{3,2},{4,5},{5,4},{6,7},{7,6},{8,9},{9,8},{10,11... | collective-permute-start | bytes 2752520 | tf_op jit(solution)/shard_map/ppermute | solution.py:500
